TPU v7x, 32 devices: a whole 2x2x4 slice. The times are simulated.
32 devices in a mesh: chan: 2 (over y), tile: 16 (over z, x, core).
Axes of the slice: x: 2, y: 2, z: 4, core: 2. Of those that a mesh axis runs over, the one named last changes fastest.
Arguments:
- sky_cube: float32 [256, 512, 1024], P('chan', 'tile'), may hold values from -8 to 8
- pixel_mask: int32 [512, 1024], P('tile'), may hold values 0 or 1
- radius: int32 [256], replicated, may hold values from 1 to 4, as said below
- chan_weight: float32 [256], replicated, may hold values from 0.5 to 2
- band: float32 [17, 256], replicated, may hold values from -0.15 to 0.15
- resample: float32 [256, 256], replicated, may hold values from -0.375 to 0.375
- slab_index: int32 [256], replicated, may hold values from 0 to 15, never falling along the last dimension, each value on 1 to 20 neighbouring positions
Outputs:
- slabs: float32 [320, 512, 1024], P('tile', None, 'chan')
Inputs may be any that keep to these rules, and one draw needn't show every extreme that they name: Every channel's radius is 1 to 4; some channel has 4. `slab_index`: never falls along the rows; each owner gets 1 to 20 rows and some owner exactly 20.
All inputs are finite; a program needn't handle non-finite values. No bound on the sum of `pixel_mask` on one device may be relied on, other than what follows from the above.
Results may differ from a plain program's by a relative error of at most 0.00007.
Values sent between devices are 32-bit elements; how exact they have to be, the bound alone decides.
No kernel may reach another device: no remote copies, remote signals or barrier semaphores. Data moves between devices by JAX's collectives and lax.ppermute only.
A program may use at most 128 MiB of HBM per device.

v0:
```python
import jax
import jax.numpy as jnp
from jax import lax
from jax.sharding import PartitionSpec as P

NCH = 256
NOUT = 256
CAP = 20
RMAX = 4
BW = 8


def padded_2(block, sides, width):
    for axis, dim in sides:
        count = lax.axis_size(axis)
        forward = [(i, i + 1) for i in range(count - 1)]
        backward = [(target, source) for source, target in forward]
        low = lax.ppermute(
            lax.slice_in_dim(block, block.shape[dim] - width, None, axis=dim), axis, forward
        )
        high = lax.ppermute(lax.slice_in_dim(block, 0, width, axis=dim), axis, backward)
        block = jnp.concatenate([low, block, high], axis=dim)
    return block


def make_taps(radius):
    spread = radius.astype(jnp.float32)[:, None]
    offsets = jnp.arange(-RMAX, RMAX + 1).astype(jnp.float32)[None, :]
    sigma = 0.5 * spread + 0.5
    values = jnp.exp(-offsets * offsets / (2.0 * sigma * sigma))
    values = jnp.where(jnp.abs(offsets) <= spread, values, jnp.zeros_like(values))
    return values / jnp.sum(values, axis=1, keepdims=True)


def pass_rows(padded, weights, length):
    result = weights[:, 0, None, None] * padded[:, 0:length, :]
    for offset in range(1, 2 * RMAX + 1):
        result = result + weights[:, offset, None, None] * padded[:, offset : offset + length, :]
    return result


def pass_cols(padded, weights, length):
    result = weights[:, 0, None, None] * padded[:, :, 0:length]
    for offset in range(1, 2 * RMAX + 1):
        result = result + weights[:, offset, None, None] * padded[:, :, offset : offset + length]
    return result


def body(sky_cube, pixel_mask, radius, chan_weight, band, resample, slab_index):
    chans_here, rows_here, all_cols = sky_cube.shape
    masked = sky_cube * pixel_mask.astype(jnp.float32)[None]
    first = lax.axis_index("chan") * chans_here
    local_radius = lax.dynamic_slice_in_dim(radius, first, chans_here)
    weights = make_taps(local_radius)
    padded = padded_2(masked, (("tile", 1),), RMAX)
    along_rows = pass_rows(padded, weights, rows_here)
    widened = jnp.pad(along_rows, ((0, 0), (0, 0), (RMAX, RMAX)))
    beam = pass_cols(widened, weights, all_cols)
    pencil = lax.all_to_all(beam, "chan", split_axis=2, concat_axis=0, tiled=True)
    cols_here = pencil.shape[2]
    flat = pencil.reshape(NCH, rows_here * cols_here)
    row_ids = jnp.arange(NCH)[:, None]
    col_ids = jnp.arange(NCH)[None, :]
    distance = col_ids - row_ids
    coupling = jnp.zeros((NCH, NCH), jnp.float32)
    for offset in range(2 * BW + 1):
        coupling = coupling + jnp.where(distance == offset - BW, band[offset][:, None], 0.0)
    identity = (distance == 0).astype(jnp.float32)
    filter_matrix = (identity - coupling) * chan_weight[None, :]
    joined = jnp.dot(
        resample, filter_matrix, precision=lax.Precision.HIGHEST, preferred_element_type=jnp.float32
    )
    comoving = jnp.dot(
        joined, flat, precision=lax.Precision.HIGHEST, preferred_element_type=jnp.float32
    )
    owner_count = lax.axis_size("tile")
    owners = jnp.arange(owner_count)
    onehot = (slab_index[None, :] == owners[:, None]).astype(jnp.int32)
    count = jnp.sum(onehot, axis=1)
    start = jnp.cumsum(count) - count
    slots = jnp.arange(CAP)
    source = start[:, None] + slots[None, :]
    valid = slots[None, :] < count[:, None]
    picked = jnp.take(comoving, jnp.clip(source, 0, NOUT - 1).reshape(-1), axis=0)
    picked = jnp.where(valid.reshape(-1)[:, None], picked, jnp.zeros_like(picked))
    outgoing = picked.reshape(owner_count, CAP, rows_here, cols_here)
    arrived = lax.all_to_all(outgoing, "tile", split_axis=0, concat_axis=2, tiled=True)
    return arrived.reshape(CAP, owner_count * rows_here, cols_here)


def solution(mesh):
    in_specs = (P("chan", "tile", None), P("tile", None), P(), P(), P(), P(), P())
    out_specs = P("tile", None, "chan")
    return jax.shard_map(body, mesh=mesh, in_specs=in_specs, out_specs=out_specs, check_vma=False)
```

profile of v0, /device:TPU:1, one launch (start us, length us, event | category | flops | bytes accessed | tf_op | source)
XLA Modules:
  0.0 967.7 jit_solution(2919702836303952813)
XLA Ops:
  0.0 0.0 copy-start
  0.0 1.0 convert_element_type.30
  1.0 0.0 copy-start.4
  1.0 15.2 %copy_multiply_fusion = f32[128,32,1024]{2,0,1:T(8,128)S(1)} fusion(f32[128,32,1024]{2,1,0:T(8,128)} %param.7, f32[32,1024]{1,0:T(8,128)S(1)} %convert_element_type.30), kind=kLoop, calls=%fused_computation.62 | loop fusion | flops 4194304 | bytes 33685504 | tf_op jit(solution)/shard_map/mul | solution.py:51
  16.2 0.0 copy-start.2
  16.2 6.2 copy-done.2
  22.4 1.8 fusion.167
  24.2 4.5 collective-permute-start
  28.7 1.9 collective-permute-start.1
  30.6 0.0 copy-done.4
  30.6 0.1 multiply_multiply_fusion
  30.7 0.1 fusion.147
  30.8 0.1 fusion.146
  30.9 43.5 %collective-permute-done = f32[128,4,1024]{2,0,1:T(8,128)} collective-permute-done((f32[128,4,1024]{2,0,1:T(8,128)}, f32[128,4,1024]{2,0,1:T(8,128)}, u32[]{:S(2)}, u32[]{:S(2)}) %collective-permute-start) | collective-permute-done | bytes 2097184 | tf_op jit(solution)/shard_map/ppermute | solution.py:18
  74.4 0.0 collective-permute-done.1
  74.4 55.4 %fusion.19 = f32[128,32,1024]{2,0,1:T(8,128)} fusion(f32[128,32,1024]{2,0,1:T(8,128)} %copy-done.2, f32[128,4,1024]{2,0,1:T(8,128)} %collective-permute-done.1, f32[128,4,1024]{2,0,1:T(8,128)} %collective-permute-done, f32[128]{0:T(128)S(1)} %get-tuple-element.27, f32[128]{0:T(128)S(1)} %get-tuple-element.28, f32[128]{0:T(128)S(1)} %get-tuple-element.29, ...), kind=kLoop, calls=%fused_computation.41 | loop fusion | flops 104857600 | bytes 37753344 | tf_op jit(solution)/shard_map/add | solution.py:38
  129.8 57.5 %fusion.8 = f32[128,32,1024]{2,0,1:T(8,128)} fusion(f32[128,32,1024]{2,0,1:T(8,128)} %fusion.19, f32[128]{0:T(128)S(1)} %get-tuple-element.27, f32[128]{0:T(128)S(1)} %get-tuple-element.28, f32[128]{0:T(128)S(1)} %get-tuple-element.29, f32[128]{0:T(128)S(1)} %get-tuple-element.30, f32[128]{0:T(128)S(1)} %get-tuple-element.31, f32[128]{0:T(128)S(1)} %get-tuple-element.32, ...), kind=kLoop, calls=%fused_computation.30 | loop fusion | flops 71303168 | bytes 33559040 | tf_op jit(solution)/shard_map/add | solution.py:45
  187.3 17.5 %copy.25 = f32[128,32,1024]{0,1,2:T(8,128)} copy(f32[128,32,1024]{2,0,1:T(8,128)} %fusion.8) | data formatting | bytes 33554432 | tf_op jit(solution)/shard_map/add | solution.py:45
  204.8 0.0 copy-start.5
  204.8 0.0 copy-start.3
  204.8 0.0 copy-start.6
  204.8 10.0 %all-to-all-start = ((f32[128,32,1024]{0,1,2:T(8,128)}), f32[128,32,1024]{0,1,2:T(8,128)}, u32[]{:S(2)}, u32[]{:S(2)}) async-start(f32[128,32,1024]{0,1,2:T(8,128)} %copy.25), calls=%async_computation | async-start | bytes 33554432 | tf_op jit(solution)/shard_map/all_to_all | solution.py:59
  214.8 0.0 copy-done.5
  214.8 0.1 convert_reduce_fusion
  214.9 0.1 copy.23
  215.0 0.1 reduce
  215.2 0.1 add_clamp_fusion
  215.2 0.1 min.12
  215.4 0.1 iota_compare_fusion.1
  215.5 0.0 copy-done.3
  215.5 0.0 copy-done
  215.5 0.0 copy-done.6
  215.5 1.2 fusion.38
  216.8 141.4 %all-to-all-done = f32[128,32,1024]{0,1,2:T(8,128)} async-done(((f32[128,32,1024]{0,1,2:T(8,128)}), f32[128,32,1024]{0,1,2:T(8,128)}, u32[]{:S(2)}, u32[]{:S(2)}) %all-to-all-start) | async-done | bytes 16777248 | tf_op jit(solution)/shard_map/all_to_all | solution.py:59
  358.2 20.2 %copy.26 = f32[128,32,2,512]{3,1,0,2:T(8,128)} copy(f32[128,32,2,512]{0,1,3,2:T(8,128)} %bitcast.27) | data formatting | bytes 33554432 | tf_op jit(solution)/shard_map/all_to_all | solution.py:59
  378.4 18.6 %copy.28 = f32[32,8,32,512]{3,1,2,0:T(8,128)} copy(f32[32,8,32,512]{3,2,1,0:T(8,128)} %bitcast.55) | data formatting | bytes 33554432
  397.0 21.9 %fusion.169 = f32[256,16384]{1,0:T(8,128)} fusion(f32[256,256]{1,0:T(8,128)S(1)} %fusion.38, f32[256,16384]{1,0:T(8,128)} %bitcast.54), kind=kOutput, calls=%fused_computation.201 | convolution fusion | flops 12884901888 | bytes 33816576 | tf_op jit(solution)/shard_map/dot_general | solution.py:73
  418.8 32.3 %gather_fusion = f32[320,16384]{1,0:T(8,128)} fusion(f32[256,16384]{1,0:T(8,128)} %fusion.169, s32[1024]{0:T(1024)S(1)} %pad_clamp_fusion), kind=kCustom, calls=%fused_computation | custom fusion | bytes 41944320 | tf_op jit(solution)/shard_map/jit(_take)/gather | solution.py:84
  451.2 21.1 %copy.29 = f32[40,8,32,512]{3,2,1,0:T(8,128)S(1)} copy(f32[40,8,32,512]{3,1,2,0:T(8,128)} %bitcast.51) | data formatting | bytes 41943040
  472.3 7.7 select_select_fusion
  480.0 479.5 %all_to_all.30 = f32[16,20,32,512]{3,2,1,0:T(8,128)S(1)} all-to-all(f32[16,20,32,512]{3,2,1,0:T(8,128)} %select_select_fusion), channel_id=1, replica_groups=mesh['chan'=2,'tile'=16] {'tile'}, dimensions={0} | all-to-all | bytes 41943040 | tf_op jit(solution)/shard_map/all_to_all | solution.py:87
  959.5 0.0 copy-start.1
  959.5 7.7 copy.27
  967.2 0.0 copy-done.1
  (7 shorter events, 0.1 us)
Async XLA Ops:
  0.0 215.5 %copy-start = (f32[256,256]{1,0:T(8,128)S(1)}, f32[256,256]{1,0:T(8,128)}, u32[]{:S(2)}) copy-start(f32[256,256]{1,0:T(8,128)} %param.12) | copy-start | bytes 786436
  1.0 29.6 %copy-start.4 = (s32[256]{0:T(256)S(1)}, s32[256]{0:T(256)}, u32[]{:S(2)}) copy-start(s32[256]{0:T(256)} %param.9) | copy-start | bytes 3076
  16.2 6.2 copy-start.2
  24.2 50.2 %collective-permute-start = (f32[128,4,1024]{2,0,1:T(8,128)}, f32[128,4,1024]{2,0,1:T(8,128)}, u32[]{:S(2)}, u32[]{:S(2)}) collective-permute-start(f32[128,4,1024]{2,0,1:T(8,128)} %get-tuple-element.7), channel_id=1, source_target_pairs={{0,1},{1,2},{2,3},{3,4},{4,5},{5,6},{6,7},{7,8},{8,9},{9,10},{10,1... | collective-permute-start | bytes 6291464 | tf_op jit(solution)/shard_map/ppermute | solution.py:18
  28.7 45.7 %collective-permute-start.1 = (f32[128,4,1024]{2,0,1:T(8,128)S(1)}, f32[128,4,1024]{2,0,1:T(8,128)}, u32[]{:S(2)}, u32[]{:S(2)}) collective-permute-start(f32[128,4,1024]{2,0,1:T(8,128)S(1)} %get-tuple-element.8), channel_id=1, source_target_pairs={{1,0},{2,1},{3,2},{4,3},{5,4},{6,5},{7,6},{8,7},{9,8},{10,9},{11,1... | collective-permute-start | bytes 6291464 | tf_op jit(solution)/shard_map/ppermute | solution.py:21
  204.8 10.0 %copy-start.5 = (s32[256]{0:T(256)S(1)}, s32[256]{0:T(256)}, u32[]{:S(2)}) copy-start(s32[256]{0:T(256)} %param.13) | copy-start | bytes 3076
  204.8 10.7 %copy-start.3 = (f32[17,256]{1,0:T(8,128)S(1)}, f32[17,256]{1,0:T(8,128)}, u32[]{:S(2)}) copy-start(f32[17,256]{1,0:T(8,128)} %param.11) | copy-start | bytes 52228
  204.8 10.7 %copy-start.6 = (f32[256]{0:T(256)S(1)}, f32[256]{0:T(256)}, u32[]{:S(2)}) copy-start(f32[256]{0:T(256)} %param.10) | copy-start | bytes 3076
  204.8 153.4 %all-to-all-start = ((f32[128,32,1024]{0,1,2:T(8,128)}), f32[128,32,1024]{0,1,2:T(8,128)}, u32[]{:S(2)}, u32[]{:S(2)}) async-start(f32[128,32,1024]{0,1,2:T(8,128)} %copy.25), calls=%async_computation | async-start | bytes 33554432 | tf_op jit(solution)/shard_map/all_to_all | solution.py:59
  959.5 7.7 copy-start.1
where the time goes:
time: 977 us; the launch traced here: 968 us
  blocking collectives  480 us (49%)
  waiting for transfers between devices  185 us (19%)
  other arithmetic  137 us (14%)
  local copies, waits for them, and re-layouts  126 us (13%)
  matrix products  23.1 us (2%)
  starting transfers between devices  16.4 us (2%)
    all_to_all x1, blocking collectives, body(): lax.all_to_all(outgoing, 'tile', split_axis=0, concat_axis=2, tiled=True)  480 us
    all_to_all x1, waiting for transfers between devices, body(): lax.all_to_all(beam, 'chan', split_axis=2, concat_axis=0, tiled=True)  141 us
    add x1, other arithmetic, pass_cols(): result + weights[:, offset, None, None] * padded[:, :, offset:offset + le...  57.5 us
    add x1, other arithmetic, pass_rows(): result + weights[:, offset, None, None] * padded[:, offset:offset + lengt...  55.4 us
    unnamed x16, local copies, waits for them, and re-layouts  45.9 us
    ppermute x1, waiting for transfers between devices, padded_2(): lax.ppermute(lax.slice_in_dim(block, block.shape[dim] - width, None, axis...  43.5 us
    gather x1, local copies, waits for them, and re-layouts, body(): jnp.take(comoving, jnp.clip(source, 0, NOUT - 1).reshape(-1), axis=0)  32.3 us
    dot_general x1, matrix products, body(): jnp.dot(joined, flat, precision=lax.Precision.HIGHEST, preferred_element_...  21.9 us
  transfers between devices with their start and end apart: 3, of which 2 were waited for; matrix products, arithmetic and copies ran while one was open for 0% of the time, Pallas kernels for 0%

commit v1 on v0

v1 whole, which is shorter than its diff:
```python
import jax
import jax.numpy as jnp
from jax import lax
from jax.experimental import pallas as pl
from jax.experimental.pallas import tpu as pltpu
from jax.sharding import PartitionSpec as P


CAP = 20
RMAX = 4
BW = 8
ROWS = 8
LANES = 128
SLOTS = 24
SUB = 256

LIGHT = pl.CostEstimate(flops=1, bytes_accessed=1, transcendentals=0)


def make_taps(radius):
    spread = radius.astype(jnp.float32)[:, None]
    offsets = jnp.arange(-RMAX, RMAX + 1).astype(jnp.float32)[None, :]
    sigma = 0.5 * spread + 0.5
    values = jnp.exp(-offsets * offsets / (2.0 * sigma * sigma))
    values = jnp.where(jnp.abs(offsets) <= spread, values, jnp.zeros_like(values))
    return (values / jnp.sum(values, axis=1, keepdims=True))[:, RMAX:]


def partner(index, step, count):
    if count & (count - 1) == 0:
        return index ^ step
    return (index + step) % count


def source_of(index, step, count):
    if count & (count - 1) == 0:
        return index ^ step
    return (index + count - step) % count


def shift(block, axis, step):
    count = lax.axis_size(axis)
    return lax.ppermute(block, axis, [(i, partner(i, step, count)) for i in range(count)])


def beam_kernel(above, below, first, last, count, col_width, pieces, waits, *refs):
    here_ref, taps_ref, prev_ref, cur_ref, next_ref, mprev_ref, mcur_ref, mnext_ref = refs[:8]
    outs = refs[8 + waits : -2]
    window, scratch = refs[-2:]
    group = cur_ref.shape[0]
    tiles = cur_ref.shape[2] // LANES
    base = pl.program_id(0) * group
    edges = list(outs[count * len(pieces) :])
    lane = lax.broadcasted_iota(jnp.int32, (ROWS, LANES), 1)
    zeros = jnp.zeros((ROWS, LANES), jnp.float32)

    def one(c, slot):
        taps = [taps_ref[(base + c) * (RMAX + 1) + k] for k in range(RMAX + 1)]
        sums = []
        for b in range(tiles):
            at = pl.ds(b * LANES, LANES)
            if above:
                window[slot, b, ROWS - RMAX : ROWS] = prev_ref[c, :, at]
            else:
                prev = prev_ref[c, :, at] * mprev_ref[:, at].astype(jnp.float32)
                window[slot, b, :ROWS] = prev
            window[slot, b, ROWS : 2 * ROWS] = cur_ref[c, :, at] * mcur_ref[:, at].astype(jnp.float32)
            if below:
                window[slot, b, 2 * ROWS : 2 * ROWS + RMAX] = next_ref[c, :, at]
            else:
                after = next_ref[c, :, at] * mnext_ref[:, at].astype(jnp.float32)
                window[slot, b, 2 * ROWS :] = after
            total = taps[0] * window[slot, b, ROWS : 2 * ROWS]
            for k in range(1, RMAX + 1):
                total = total + taps[k] * (
                    window[slot, b, ROWS - k : 2 * ROWS - k] + window[slot, b, ROWS + k : 2 * ROWS + k]
                )
            sums.append(total)
            if first:
                edges[0][c, :, at] = window[slot, b, :RMAX]
            if last:
                edges[-1][c, :, at] = window[slot, b, 3 * ROWS - RMAX :]
        totals = [taps[0] * total for total in sums]
        for k in range(1, RMAX + 1):
            right = [pltpu.roll(total, k, 1) for total in sums]
            left = [pltpu.roll(total, LANES - k, 1) for total in sums]
            for b in range(tiles):
                below_ = right[b - 1] if b else zeros
                above_ = left[b + 1] if b + 1 < tiles else zeros
                totals[b] = totals[b] + taps[k] * (
                    jnp.where(lane < k, below_, right[b])
                    + jnp.where(lane >= LANES - k, above_, left[b])
                )
        for b in range(tiles):
            scratch[c, :, pl.ds(b * LANES, LANES)] = totals[b]

    def pair(i, carry):
        one(2 * i, 0)
        one(2 * i + 1, 1)
        return carry

    lax.fori_loop(0, group // 2, pair, 0)
    me = here_ref[0]
    at = 0
    for step in range(count):
        start = partner(me, step, count) * col_width
        for col, width in pieces:
            outs[at][...] = scratch[:, :, pl.ds(pl.multiple_of(start + col, LANES), width)]
            at += 1


def beam_block(sky, mask, up, down, taps, me, block, count, pieces, after):
    chans, rows, cols = sky.shape
    blocks = rows // ROWS
    above, below = block == 0, block == blocks - 1
    first, last = block == 1 and blocks > 2, block == blocks - 2 and blocks > 2
    group = min(chans, 16)
    col_width = cols // count
    full = lambda b: pl.BlockSpec((group, ROWS, cols), lambda i: (i, b, 0))
    half = pl.BlockSpec((group, RMAX, cols), lambda i: (i, 0, 0))
    mrow = lambda b: pl.BlockSpec((ROWS, cols), lambda i: (b, 0))
    lo, hi = max(block - 1, 0), min(block + 1, blocks - 1)
    smem = pl.BlockSpec(memory_space=pltpu.SMEM)
    out_specs, out_shapes = [], []
    for _ in range(count):
        for _, width in pieces:
            out_specs.append(pl.BlockSpec((group, ROWS, width), lambda i: (i, 0, 0)))
            out_shapes.append(jax.ShapeDtypeStruct((chans, ROWS, width), jnp.float32))
    for _ in range(first + last):
        out_specs.append(half)
        out_shapes.append(jax.ShapeDtypeStruct((chans, RMAX, cols), jnp.float32))
    return pl.pallas_call(
        lambda *refs: beam_kernel(
            above, below, first, last, count, col_width, pieces, len(after), *refs
        ),
        grid=(chans // group,),
        in_specs=[
            smem,
            smem,
            half if above else full(lo),
            full(block),
            half if below else full(hi),
            mrow(lo),
            mrow(block),
            mrow(hi),
        ]
        + [pl.BlockSpec(memory_space=pl.ANY)] * len(after),
        out_specs=out_specs,
        out_shape=out_shapes,
        scratch_shapes=[
            pltpu.VMEM((2, cols // LANES, 3 * ROWS, LANES), jnp.float32),
            pltpu.VMEM((group, ROWS, cols), jnp.float32),
        ],
        cost_estimate=LIGHT,
        name="beam",
    )(me, taps, up if above else sky, sky, down if below else sky, mask, mask, mask, *after)


def mix_kernel(count, owners, waits, weights_ref, *refs):
    parts, outs = refs[:count], refs[count + waits :]
    chans = parts[0].shape[0]
    columns = []
    for part in parts:
        flat = part.reshape(chans * ROWS, LANES)
        columns.append(
            jnp.concatenate([flat[pl.ds(r, chans, stride=ROWS), :] for r in range(ROWS)], axis=1)
        )
    values = jnp.concatenate(columns, axis=0)
    high = values.astype(jnp.bfloat16)
    low = (values - high.astype(jnp.float32)).astype(jnp.bfloat16)
    mixed = jnp.dot(
        weights_ref[...],
        jnp.concatenate([high, high, low], axis=0),
        preferred_element_type=jnp.float32,
    )
    for o in range(owners):
        flat = outs[o].reshape(CAP * ROWS, LANES)
        for r in range(ROWS):
            flat[pl.ds(r, CAP, stride=ROWS), :] = mixed[
                o * SLOTS : o * SLOTS + CAP, r * LANES : (r + 1) * LANES
            ]


def mix(weights, parts, owners, after):
    count = len(parts)
    chans, _, width = parts[0].shape
    k = weights.shape[0] * weights.shape[1] * ROWS * width
    return pl.pallas_call(
        lambda *refs: mix_kernel(count, owners, len(after), *refs),
        grid=(width // LANES,),
        in_specs=[pl.BlockSpec(weights.shape, lambda j: (0, 0))]
        + [pl.BlockSpec((chans, ROWS, LANES), lambda j: (0, 0, j))] * count
        + [pl.BlockSpec(memory_space=pl.ANY)] * len(after),
        out_specs=[pl.BlockSpec((CAP, ROWS, LANES), lambda j: (0, 0, j))] * owners,
        out_shape=[jax.ShapeDtypeStruct((CAP, ROWS, width), jnp.float32)] * owners,
        cost_estimate=pl.CostEstimate(
            flops=2 * k, bytes_accessed=4 * ROWS * width * (count * chans + owners * CAP), transcendentals=0
        ),
        name="mix",
    )(weights, *parts, *after)


def place_kernel(owners, rows, block, col, width, aliased, here_ref, *refs):
    arrived = refs[:owners][::-1]
    out, buffer, sems = refs[owners + aliased :]
    me = here_ref[0]
    loads = [pltpu.make_async_copy(arrived[m], buffer.at[m], sems.at[m]) for m in range(owners)]
    for load in loads:
        load.start()
    stores = []
    for m in range(owners):
        loads[m].wait()
        row = pl.multiple_of(source_of(me, m, owners) * rows + block * ROWS, ROWS)
        store = pltpu.make_async_copy(
            buffer.at[m], out.at[:, pl.ds(row, ROWS), pl.ds(col, width)], sems.at[owners + m]
        )
        store.start()
        stores.append(store)
    for store in stores:
        store.wait()


def place(result, shape, arrived, me, rows, block, col):
    owners = len(arrived)
    width = arrived[0].shape[2]
    aliased = 0 if result is None else 1
    anywhere = pl.BlockSpec(memory_space=pl.ANY)
    return pl.pallas_call(
        lambda *refs: place_kernel(owners, rows, block, col, width, aliased, *refs),
        in_specs=[pl.BlockSpec(memory_space=pltpu.SMEM)] + [anywhere] * (owners + aliased),
        out_specs=anywhere,
        out_shape=jax.ShapeDtypeStruct(shape, jnp.float32),
        scratch_shapes=[
            pltpu.VMEM((owners, CAP, ROWS, width), jnp.float32),
            pltpu.SemaphoreType.DMA((2 * owners,)),
        ],
        input_output_aliases={owners + 1: 0} if aliased else {},
        cost_estimate=LIGHT,
        name="place",
    )(me, *arrived[::-1], *([result] if aliased else []))


def mixing_weights(resample, band, chan_weight, slab_index, me_chan, me_tile, chans, owners):
    nch = resample.shape[1]
    row_ids = jnp.arange(nch)[:, None]
    col_ids = jnp.arange(nch)[None, :]
    distance = col_ids - row_ids
    coupling = jnp.zeros((nch, nch), jnp.float32)
    for offset in range(2 * BW + 1):
        coupling = coupling + jnp.where(distance == offset - BW, band[offset][:, None], 0.0)
    identity = (distance == 0).astype(jnp.float32)
    filter_matrix = (identity - coupling) * chan_weight[None, :]
    joined = jnp.dot(
        resample, filter_matrix, precision=lax.Precision.HIGHEST, preferred_element_type=jnp.float32
    )
    line = jnp.arange(owners * SLOTS)
    owner = partner(me_tile, line // SLOTS, owners)
    slot = line % SLOTS
    start = jnp.sum((slab_index[None, :] < owner[:, None]).astype(jnp.int32), axis=1)
    row = jnp.arange(resample.shape[0])[None, :]
    chosen = (
        (slab_index[None, :] == owner[:, None])
        & (row - start[:, None] == slot[:, None])
        & (slot[:, None] < CAP)
    ).astype(jnp.float32)
    count = nch // chans
    order = jnp.concatenate(
        [
            lax.dynamic_slice_in_dim(joined, source_of(me_chan, step, count) * chans, chans, axis=1)
            for step in range(count)
        ],
        axis=1,
    )
    weights = jnp.dot(
        chosen, order, precision=lax.Precision.HIGHEST, preferred_element_type=jnp.float32
    )
    high = lax.reduce_precision(weights, exponent_bits=8, mantissa_bits=7)
    low = weights - high
    return jnp.concatenate([high, low, high], axis=1).astype(jnp.bfloat16)


def body(sky_cube, pixel_mask, radius, chan_weight, band, resample, slab_index):
    chans, rows, cols = sky_cube.shape
    nchan, owners = lax.axis_size("chan"), lax.axis_size("tile")
    me_chan, me_tile = lax.axis_index("chan"), lax.axis_index("tile")
    col_width = cols // nchan
    blocks = rows // ROWS

    taps = make_taps(lax.dynamic_slice_in_dim(radius, me_chan * chans, chans)).reshape(-1)
    here_chan = jnp.reshape(me_chan, (1,)).astype(jnp.int32)
    here_tile = jnp.reshape(me_tile, (1,)).astype(jnp.int32)

    sub = min(SUB, col_width)
    fine = tuple((c, sub) for c in range(0, col_width, sub))
    whole = ((0, col_width),)
    order = list(range(1, blocks - 1)) + [0] + ([blocks - 1] if blocks > 1 else [])
    weights = mixing_weights(
        resample, band, chan_weight, slab_index, me_chan, me_tile, chans, owners
    )
    shape = (CAP, owners * rows, col_width)
    forward = [(i, i + 1) for i in range(owners - 1)]
    backward = [(b, a) for a, b in forward]
    edges = {}
    if blocks <= 2:
        mask = pixel_mask.astype(jnp.float32)[None]
        edges["first"] = sky_cube[:, :RMAX] * mask[:, :RMAX]
        edges["last"] = sky_cube[:, rows - RMAX :] * mask[:, rows - RMAX :]
    up = down = result = None
    mixed, placed = [], []
    for at, block in enumerate(order):
        pieces = fine if at in (0, len(order) - 1) else whole
        after = mixed[at - 2 : at - 1] if at >= 2 else []
        if block == 0 and up is None:
            up = lax.ppermute(edges["last"], "tile", forward)
        if block == blocks - 1 and down is None:
            down = lax.ppermute(edges["first"], "tile", backward)
        cut = beam_block(sky_cube, pixel_mask, up, down, taps, here_chan, block, nchan, pieces, after)
        extra = list(cut[nchan * len(pieces) :])
        if blocks > 2 and block == 1:
            edges["first"] = extra[0]
        if blocks > 2 and block == blocks - 2:
            edges["last"] = extra[-1]
        for j, (col, _) in enumerate(pieces):
            parts = [cut[j]]
            for step in range(1, nchan):
                parts.append(shift(cut[step * len(pieces) + j], "chan", step))
            outgoing = mix(weights, parts, owners, placed[-2:-1])
            mixed.append(outgoing[0])
            arrived = {0: outgoing[0]}
            for m in range(owners - 1, 0, -1):
                arrived[m] = shift(outgoing[m], "tile", m)
            arrived = [arrived[m] for m in range(owners)]
            result = place(result, shape, arrived, here_tile, rows, block, col)
            placed.append(result)
    return result


def solution(mesh):
    in_specs = (P("chan", "tile", None), P("tile", None), P(), P(), P(), P(), P())
    out_specs = P("tile", None, "chan")

    return jax.shard_map(body, mesh=mesh, in_specs=in_specs, out_specs=out_specs, check_vma=False)
```

time: 977 us -> 756 us (0.77)
  blocking collectives: 480 us -> 0 us
  starting transfers between devices: 16.4 us -> 311 us
  other arithmetic: 137 us -> 2.23 us
  Pallas kernels: 0 us -> 125 us
  waiting for transfers between devices: 185 us -> 307 us
  local copies, waits for them, and re-layouts: 126 us -> 6.48 us
  matrix products: 23.1 us -> 1.74 us
    all_to_all x1 -> x0, blocking collectives: 480 us -> none  [body(): lax.all_to_all(outgoing, 'tile', split_axis=0, concat_axis=2, tiled=True)]
    ppermute x2 -> x98, starting transfers between devices: 6.41 us -> 311 us  [the longest x96 302 us: shift(): lax.ppermute(block, axis, [(i, partner(i, step, count)) for i in range(co...]
    ppermute x2 -> x98, waiting for transfers between devices: 43.5 us -> 307 us  [the longest x96 307 us: shift(): lax.ppermute(block, axis, [(i, partner(i, step, count)) for i in range(co...]
    all_to_all x1 -> x0, waiting for transfers between devices: 141 us -> none  [body(): lax.all_to_all(beam, 'chan', split_axis=2, concat_axis=0, tiled=True)]
    pallas_call x0 -> x16, Pallas kernels: none -> 125 us  [the longest x4 73 us: beam_block(): pl.pallas_call(lambda *refs: beam_kernel(above, below, first, last, count...]
    add x2 -> x0, other arithmetic: 113 us -> none  [the longest x1 57.5 us: pass_cols(): result + weights[:, offset, None, None] * padded[:, :, offset:offset + le...]
    unnamed x16 -> x154, local copies, waits for them, and re-layouts: 45.9 us -> 5.64 us
    gather x1 -> x0, local copies, waits for them, and re-layouts: 32.3 us -> none  [body(): jnp.take(comoving, jnp.clip(source, 0, NOUT - 1).reshape(-1), axis=0)]
  transfers between devices with their start and end apart: 3 -> 98, of which waited for: 2 -> 47; matrix products, arithmetic and copies ran while one was open for 0% -> 0% of each run, Pallas kernels for 0% -> 14%
where the time goes in v1:
time: 756 us; the launch traced here: 755 us
  starting transfers between devices  311 us (41%)
  waiting for transfers between devices  307 us (41%)
  Pallas kernels  125 us (17%)
    ppermute x96, waiting for transfers between devices, shift(): lax.ppermute(block, axis, [(i, partner(i, step, count)) for i in range(co...  307 us
    ppermute x96, starting transfers between devices, shift(): lax.ppermute(block, axis, [(i, partner(i, step, count)) for i in range(co...  302 us
    pallas_call x4, Pallas kernels, beam_block(): pl.pallas_call(lambda *refs: beam_kernel(above, below, first, last, count...  73 us
    pallas_call x6, Pallas kernels, mix(): pl.pallas_call(lambda *refs: mix_kernel(count, owners, len(after), *refs)...  31.1 us
    pallas_call x6, Pallas kernels, place(): pl.pallas_call(lambda *refs: place_kernel(owners, rows, block, col, width...  21.1 us
  transfers between devices with their start and end apart: 98, of which 47 were waited for; matrix products, arithmetic and copies ran while one was open for 0% of the time, Pallas kernels for 14%

profile of v1, /device:TPU:1, one launch (start us, length us, event | category | flops | bytes accessed | tf_op | source)
XLA Modules:
  0.0 754.6 jit_solution(4739750692811102091)
XLA Ops:
  1.9 18.6 %beam.4 = (f32[128,8,256]{2,1,0:T(8,128)}, f32[128,8,256]{2,1,0:T(8,128)}, f32[128,8,256]{2,1,0:T(8,128)}, f32[128,8,256]{2,1,0:T(8,128)}, f32[128,4,1024]{2,1,0:T(4,128)}) custom-call(s32[1]{0:T(128)} %bitcast.20.refs_0_, f32[640]{0:T(1024)} %reshape.75.refs_1_, f32[128,32,1024]{2,1,0:T(8,128)} %refs_4_.5, f32[128,32,1024]{2,1,0:T(8,128)} %refs_4_.5, ...), custom_call_target="tpu_custom_call" | custom-call | flops 1 | bytes 1 | tf_op jit(solution)/shard_map/beam/pallas_call | solution.py:132
  22.7 18.6 %beam.6 = (f32[128,8,512]{2,1,0:T(8,128)}, f32[128,8,512]{2,1,0:T(8,128)}, f32[128,4,1024]{2,1,0:T(4,128)}) custom-call(s32[1]{0:T(128)} %bitcast.20.refs_0_, f32[640]{0:T(1024)} %reshape.75.refs_1_, f32[128,32,1024]{2,1,0:T(8,128)} %refs_4_.5, f32[128,32,1024]{2,1,0:T(8,128)} %refs_4_.5, f32[128,32,1024]{2,1,0:T(8,128)} %refs_4_.5, s32[32,1024]{1,0:T(8,128)} %refs_7_.7, ...), custom_call_target="tpu_custom_call" | custom-call | flops 1 | bytes 1 | tf_op jit(solution)/shard_map/beam/pallas_call | solution.py:132
  42.7 4.5 collective-permute-start.3
  51.3 4.3 mix.7
  59.3 54.0 %collective-permute-done.1.refs_2_ = f32[128,8,256]{2,1,0:T(8,128)} collective-permute-done((f32[128,8,256]{2,1,0:T(8,128)}, f32[128,8,256]{2,1,0:T(8,128)}, u32[]{:S(2)}, u32[]{:S(2)}) %collective-permute-start.1) | collective-permute-done | bytes 1048608 | tf_op jit(solution)/shard_map/ppermute | solution.py:43
  113.3 4.7 collective-permute-start.23
  118.5 4.0 collective-permute-done.23.refs_3_
  122.5 10.7 %collective-permute-start.26 = (f32[20,8,256]{2,1,0:T(8,128)}, f32[20,8,256]{2,1,0:T(8,128)S(1)}, u32[]{:S(2)}, u32[]{:S(2)}) collective-permute-start(f32[20,8,256]{2,1,0:T(8,128)} %get-tuple-element.147), channel_id=1, source_target_pairs={{0,10},{1,11},{2,8},{3,9},{4,14},{5,15},{6,12},{7,13},{8,2},{9,3},... | collective-permute-start | bytes 491528 | tf_op jit(solution)/shard_map/ppermute | solution.py:43
  133.2 4.4 collective-permute-start
  137.6 6.4 collective-permute-done.25.refs_5_
  144.0 10.5 %collective-permute-done.26.refs_6_ = f32[20,8,256]{2,1,0:T(8,128)S(1)} collective-permute-done((f32[20,8,256]{2,1,0:T(8,128)}, f32[20,8,256]{2,1,0:T(8,128)S(1)}, u32[]{:S(2)}, u32[]{:S(2)}) %collective-permute-start.26) | collective-permute-done | bytes 163872 | tf_op jit(solution)/shard_map/ppermute | solution.py:43
  154.5 27.9 %collective-permute-done.27.refs_7_ = f32[20,8,256]{2,1,0:T(8,128)S(1)} collective-permute-done((f32[20,8,256]{2,1,0:T(8,128)}, f32[20,8,256]{2,1,0:T(8,128)S(1)}, u32[]{:S(2)}, u32[]{:S(2)}) %collective-permute-start.27) | collective-permute-done | bytes 163872 | tf_op jit(solution)/shard_map/ppermute | solution.py:43
  182.5 7.6 %collective-permute-done.29.refs_9_ = f32[20,8,256]{2,1,0:T(8,128)} collective-permute-done((f32[20,8,256]{2,1,0:T(8,128)}, f32[20,8,256]{2,1,0:T(8,128)}, u32[]{:S(2)}, u32[]{:S(2)}) %collective-permute-start.29) | collective-permute-done | bytes 163872 | tf_op jit(solution)/shard_map/ppermute | solution.py:43
  190.1 6.2 collective-permute-done.31.refs_11_
  196.9 6.2 collective-permute-done.33.refs_13_
  203.2 4.3 mix.6
  207.6 3.6 collective-permute-start.11
  211.3 10.6 %collective-permute-done.10.refs_5_ = f32[20,8,256]{2,1,0:T(8,128)} collective-permute-done((f32[20,8,256]{2,1,0:T(8,128)}, f32[20,8,256]{2,1,0:T(8,128)}, u32[]{:S(2)}, u32[]{:S(2)}) %collective-permute-start.10) | collective-permute-done | bytes 163872 | tf_op jit(solution)/shard_map/ppermute | solution.py:43
  221.9 10.5 %collective-permute-done.11.refs_6_ = f32[20,8,256]{2,1,0:T(8,128)} collective-permute-done((f32[20,8,256]{2,1,0:T(8,128)}, f32[20,8,256]{2,1,0:T(8,128)}, u32[]{:S(2)}, u32[]{:S(2)}) %collective-permute-start.11) | collective-permute-done | bytes 163872 | tf_op jit(solution)/shard_map/ppermute | solution.py:43
  238.4 18.0 %beam.7 = (f32[128,8,512]{2,1,0:T(8,128)}, f32[128,8,512]{2,1,0:T(8,128)}) custom-call(s32[1]{0:T(128)} %bitcast.20.refs_0_, f32[640]{0:T(1024)} %reshape.75.refs_1_, f32[128,4,1024]{2,1,0:T(4,128)} %collective-permute-done.3.refs_2_, f32[128,32,1024]{2,1,0:T(8,128)} %refs_4_.5, f32[128,32,1024]{2,1,0:T(8,128)} %refs_4_.5, s32[32,1024]{1,0:T(8,128)} %refs_7_.7, ...), custom_call_target="tpu_custom_call" | custom-call | flops 1 | bytes 1 | tf_op jit(solution)/shard_map/beam/pallas_call | solution.py:132
  259.9 4.8 collective-permute-done.16.refs_11_
  277.1 5.1 collective-permute-start.7
  283.5 3.9 collective-permute-start.9
  287.5 6.9 mix.9
  303.8 3.7 collective-permute-done.52.refs_1_
  307.5 34.2 %collective-permute-start.56 = (f32[20,8,512]{2,1,0:T(8,128)}, f32[20,8,512]{2,1,0:T(8,128)S(1)}, u32[]{:S(2)}, u32[]{:S(2)}) collective-permute-start(f32[20,8,512]{2,1,0:T(8,128)} %get-tuple-element.179), channel_id=1, source_target_pairs={{0,11},{1,10},{2,9},{3,8},{4,15},{5,14},{6,13},{7,12},{8,3},{9,2},... | collective-permute-start | bytes 983048 | tf_op jit(solution)/shard_map/ppermute | solution.py:43
  341.7 13.5 %collective-permute-start.57 = (f32[20,8,512]{2,1,0:T(8,128)}, f32[20,8,512]{2,1,0:T(8,128)S(1)}, u32[]{:S(2)}, u32[]{:S(2)}) collective-permute-start(f32[20,8,512]{2,1,0:T(8,128)} %get-tuple-element.180), channel_id=1, source_target_pairs={{0,10},{1,11},{2,8},{3,9},{4,14},{5,15},{6,12},{7,13},{8,2},{9,3},... | collective-permute-start | bytes 983048 | tf_op jit(solution)/shard_map/ppermute | solution.py:43
  355.1 13.7 %collective-permute-start.58 = (f32[20,8,512]{2,1,0:T(8,128)}, f32[20,8,512]{2,1,0:T(8,128)S(1)}, u32[]{:S(2)}, u32[]{:S(2)}) collective-permute-start(f32[20,8,512]{2,1,0:T(8,128)} %get-tuple-element.181), channel_id=1, source_target_pairs={{0,9},{1,8},{2,11},{3,10},{4,13},{5,12},{6,15},{7,14},{8,1},{9,0},... | collective-permute-start | bytes 983048 | tf_op jit(solution)/shard_map/ppermute | solution.py:43
  368.8 13.5 %collective-permute-start.59 = (f32[20,8,512]{2,1,0:T(8,128)}, f32[20,8,512]{2,1,0:T(8,128)}, u32[]{:S(2)}, u32[]{:S(2)}) collective-permute-start(f32[20,8,512]{2,1,0:T(8,128)} %get-tuple-element.182), channel_id=1, source_target_pairs={{0,8},{1,9},{2,10},{3,11},{4,12},{5,13},{6,14},{7,15},{8,0},{9,1},... | collective-permute-start | bytes 983048 | tf_op jit(solution)/shard_map/ppermute | solution.py:43
  382.3 17.8 %beam.5 = (f32[128,8,256]{2,1,0:T(8,128)}, f32[128,8,256]{2,1,0:T(8,128)}, f32[128,8,256]{2,1,0:T(8,128)}, f32[128,8,256]{2,1,0:T(8,128)}) custom-call(s32[1]{0:T(128)} %bitcast.20.refs_0_, f32[640]{0:T(1024)} %reshape.75.refs_1_, f32[128,32,1024]{2,1,0:T(8,128)} %refs_4_.5, f32[128,32,1024]{2,1,0:T(8,128)} %refs_4_.5, ...), custom_call_target="tpu_custom_call" | custom-call | flops 1 | bytes 1 | tf_op jit(solution)/shard_map/beam/pallas_call | solution.py:132
  403.4 6.2 collective-permute-done.58.refs_7_
  409.7 7.6 %collective-permute-done.59.refs_8_ = f32[20,8,512]{2,1,0:T(8,128)} collective-permute-done((f32[20,8,512]{2,1,0:T(8,128)}, f32[20,8,512]{2,1,0:T(8,128)}, u32[]{:S(2)}, u32[]{:S(2)}) %collective-permute-start.59) | collective-permute-done | bytes 327712 | tf_op jit(solution)/shard_map/ppermute | solution.py:43
  417.5 6.9 collective-permute-done.60.refs_9_
  424.5 7.0 collective-permute-done.61.refs_10_
  431.5 6.8 collective-permute-done.62.refs_11_
  439.1 6.2 collective-permute-done.63.refs_12_
  449.4 7.0 mix.8
  456.4 4.9 place.8.refs_17_.refs_3_
  462.3 4.3 mix.11
  476.2 15.6 %collective-permute-start.88 = (f32[20,8,256]{2,1,0:T(8,128)}, f32[20,8,256]{2,1,0:T(8,128)S(1)}, u32[]{:S(2)}, u32[]{:S(2)}) collective-permute-start(f32[20,8,256]{2,1,0:T(8,128)} %get-tuple-element.214), channel_id=1, source_target_pairs={{0,10},{1,11},{2,8},{3,9},{4,14},{5,15},{6,12},{7,13},{8,2},{9,3},... | collective-permute-start | bytes 491528 | tf_op jit(solution)/shard_map/ppermute | solution.py:43
  491.8 3.7 collective-permute-start.89
  495.6 9.4 %collective-permute-start.90 = (f32[20,8,256]{2,1,0:T(8,128)}, f32[20,8,256]{2,1,0:T(8,128)S(1)}, u32[]{:S(2)}, u32[]{:S(2)}) collective-permute-start(f32[20,8,256]{2,1,0:T(8,128)} %get-tuple-element.216), channel_id=1, source_target_pairs={{0,8},{1,9},{2,10},{3,11},{4,12},{5,13},{6,14},{7,15},{8,0},{9,1},... | collective-permute-start | bytes 491528 | tf_op jit(solution)/shard_map/ppermute | solution.py:43
  505.0 7.8 %collective-permute-start.91 = (f32[20,8,256]{2,1,0:T(8,128)}, f32[20,8,256]{2,1,0:T(8,128)S(1)}, u32[]{:S(2)}, u32[]{:S(2)}) collective-permute-start(f32[20,8,256]{2,1,0:T(8,128)} %get-tuple-element.217), channel_id=1, source_target_pairs={{0,7},{1,6},{2,5},{3,4},{4,3},{5,2},{6,1},{7,0},{8,15},{9,14},{10,... | collective-permute-start | bytes 491528 | tf_op jit(solution)/shard_map/ppermute | solution.py:43
  518.0 3.5 collective-permute-start.36
  524.2 14.6 %collective-permute-done.90.refs_8_ = f32[20,8,256]{2,1,0:T(8,128)S(1)} collective-permute-done((f32[20,8,256]{2,1,0:T(8,128)}, f32[20,8,256]{2,1,0:T(8,128)S(1)}, u32[]{:S(2)}, u32[]{:S(2)}) %collective-permute-start.90) | collective-permute-done | bytes 163872 | tf_op jit(solution)/shard_map/ppermute | solution.py:43
  545.6 23.5 %collective-permute-start.41 = (f32[20,8,512]{2,1,0:T(8,128)}, f32[20,8,512]{2,1,0:T(8,128)S(1)}, u32[]{:S(2)}, u32[]{:S(2)}) collective-permute-start(f32[20,8,512]{2,1,0:T(8,128)} %get-tuple-element.162), channel_id=1, source_target_pairs={{0,10},{1,11},{2,8},{3,9},{4,14},{5,15},{6,12},{7,13},{8,2},{9,3},... | collective-permute-start | bytes 983048 | tf_op jit(solution)/shard_map/ppermute | solution.py:43
  569.1 14.3 %collective-permute-start.42 = (f32[20,8,512]{2,1,0:T(8,128)}, f32[20,8,512]{2,1,0:T(8,128)S(1)}, u32[]{:S(2)}, u32[]{:S(2)}) collective-permute-start(f32[20,8,512]{2,1,0:T(8,128)} %get-tuple-element.163), channel_id=1, source_target_pairs={{0,9},{1,8},{2,11},{3,10},{4,13},{5,12},{6,15},{7,14},{8,1},{9,0},... | collective-permute-start | bytes 983048 | tf_op jit(solution)/shard_map/ppermute | solution.py:43
  583.4 12.9 %collective-permute-start.43 = (f32[20,8,512]{2,1,0:T(8,128)}, f32[20,8,512]{2,1,0:T(8,128)}, u32[]{:S(2)}, u32[]{:S(2)}) collective-permute-start(f32[20,8,512]{2,1,0:T(8,128)} %get-tuple-element.164), channel_id=1, source_target_pairs={{0,8},{1,9},{2,10},{3,11},{4,12},{5,13},{6,14},{7,15},{8,0},{9,1},... | collective-permute-start | bytes 983048 | tf_op jit(solution)/shard_map/ppermute | solution.py:43
  596.3 14.9 %collective-permute-start.44 = (f32[20,8,512]{2,1,0:T(8,128)}, f32[20,8,512]{2,1,0:T(8,128)}, u32[]{:S(2)}, u32[]{:S(2)}) collective-permute-start(f32[20,8,512]{2,1,0:T(8,128)} %get-tuple-element.165), channel_id=1, source_target_pairs={{0,7},{1,6},{2,5},{3,4},{4,3},{5,2},{6,1},{7,0},{8,15},{9,14},{10,... | collective-permute-start | bytes 983048 | tf_op jit(solution)/shard_map/ppermute | solution.py:43
  611.2 6.3 collective-permute-done.40.refs_5_
  617.5 5.9 collective-permute-done.41.refs_6_
  623.4 8.2 %collective-permute-done.42.refs_7_ = f32[20,8,512]{2,1,0:T(8,128)S(1)} collective-permute-done((f32[20,8,512]{2,1,0:T(8,128)}, f32[20,8,512]{2,1,0:T(8,128)S(1)}, u32[]{:S(2)}, u32[]{:S(2)}) %collective-permute-start.42) | collective-permute-done | bytes 327712 | tf_op jit(solution)/shard_map/ppermute | solution.py:43
  631.6 5.6 collective-permute-done.43.refs_8_
  638.8 6.3 collective-permute-done.44.refs_9_
  646.0 6.2 collective-permute-done.45.refs_10_
  652.8 6.3 collective-permute-done.46.refs_11_
  659.1 6.8 collective-permute-done.47.refs_12_
  668.1 4.9 place.9.refs_3_.refs_17_
  673.1 4.3 mix.10
  687.0 17.8 %collective-permute-start.72 = (f32[20,8,256]{2,1,0:T(8,128)}, f32[20,8,256]{2,1,0:T(8,128)S(1)}, u32[]{:S(2)}, u32[]{:S(2)}) collective-permute-start(f32[20,8,256]{2,1,0:T(8,128)} %get-tuple-element.196), channel_id=1, source_target_pairs={{0,10},{1,11},{2,8},{3,9},{4,14},{5,15},{6,12},{7,13},{8,2},{9,3},... | collective-permute-start | bytes 491528 | tf_op jit(solution)/shard_map/ppermute | solution.py:43
  704.7 3.5 collective-permute-start.73
  708.3 9.6 %collective-permute-start.74 = (f32[20,8,256]{2,1,0:T(8,128)}, f32[20,8,256]{2,1,0:T(8,128)S(1)}, u32[]{:S(2)}, u32[]{:S(2)}) collective-permute-start(f32[20,8,256]{2,1,0:T(8,128)} %get-tuple-element.198), channel_id=1, source_target_pairs={{0,8},{1,9},{2,10},{3,11},{4,12},{5,13},{6,14},{7,15},{8,0},{9,1},... | collective-permute-start | bytes 491528 | tf_op jit(solution)/shard_map/ppermute | solution.py:43
  717.9 4.4 collective-permute-start.75
  722.3 6.3 collective-permute-done.71.refs_5_
  (315 shorter events, 121.0 us)
Async XLA Ops:
  20.6 29.7 %collective-permute-start.4 = (f32[128,8,256]{2,1,0:T(8,128)}, f32[128,8,256]{2,1,0:T(8,128)S(1)}, u32[]{:S(2)}, u32[]{:S(2)}) collective-permute-start(f32[128,8,256]{2,1,0:T(8,128)} %get-tuple-element.123), channel_id=1, source_target_pairs={{0,16},{16,0},{1,17},{17,1},{2,18},{18,2},{3,19},{19,3},{4,20},{20... | collective-permute-start | bytes 3145736 | tf_op jit(solution)/shard_map/ppermute | solution.py:43
  41.3 242.2 %collective-permute-start.51 = (f32[128,8,512]{2,1,0:T(8,128)}, f32[128,8,512]{2,1,0:T(8,128)S(1)}, u32[]{:S(2)}, u32[]{:S(2)}) collective-permute-start(f32[128,8,512]{2,1,0:T(8,128)} %get-tuple-element.174), channel_id=1, source_target_pairs={{0,16},{16,0},{1,17},{17,1},{2,18},{18,2},{3,19},{19,3},{4,20},{20... | collective-permute-start | bytes 6291464 | tf_op jit(solution)/shard_map/ppermute | solution.py:43
  41.3 72.0 %collective-permute-start.1 = (f32[128,8,256]{2,1,0:T(8,128)}, f32[128,8,256]{2,1,0:T(8,128)}, u32[]{:S(2)}, u32[]{:S(2)}) collective-permute-start(f32[128,8,256]{2,1,0:T(8,128)} %get-tuple-element.117), channel_id=1, source_target_pairs={{0,16},{16,0},{1,17},{17,1},{2,18},{18,2},{3,19},{19,3},{4,20},{20... | collective-permute-start | bytes 3145736 | tf_op jit(solution)/shard_map/ppermute | solution.py:43
  42.7 193.0 %collective-permute-start.3 = (f32[128,4,1024]{2,1,0:T(4,128)}, f32[128,4,1024]{2,1,0:T(4,128)}, u32[]{:S(2)}, u32[]{:S(2)}) collective-permute-start(f32[128,4,1024]{2,1,0:T(4,128)} %get-tuple-element.121), channel_id=1, source_target_pairs={{0,1},{1,2},{2,3},{3,4},{4,5},{5,6},{6,7},{7,8},{8,9},{9,10},{10,1... | collective-permute-start | bytes 6291464 | tf_op jit(solution)/shard_map/ppermute | solution.py:314
  55.6 62.4 %collective-permute-start.21 = (f32[20,8,256]{2,1,0:T(8,128)}, f32[20,8,256]{2,1,0:T(8,128)S(1)}, u32[]{:S(2)}, u32[]{:S(2)}) collective-permute-start(f32[20,8,256]{2,1,0:T(8,128)} %get-tuple-element.142), channel_id=1, source_target_pairs={{0,15},{1,14},{2,13},{3,12},{4,11},{5,10},{6,9},{7,8},{8,7},{9,6},... | collective-permute-start | bytes 491528 | tf_op jit(solution)/shard_map/ppermute | solution.py:43
  58.7 59.3 %collective-permute-start.22 = (f32[20,8,256]{2,1,0:T(8,128)}, f32[20,8,256]{2,1,0:T(8,128)S(1)}, u32[]{:S(2)}, u32[]{:S(2)}) collective-permute-start(f32[20,8,256]{2,1,0:T(8,128)} %get-tuple-element.143), channel_id=1, source_target_pairs={{0,14},{1,15},{2,12},{3,13},{4,10},{5,11},{6,8},{7,9},{8,6},{9,7},... | collective-permute-start | bytes 491528 | tf_op jit(solution)/shard_map/ppermute | solution.py:43
  118.0 26.0 %collective-permute-start.25 = (f32[20,8,256]{2,1,0:T(8,128)}, f32[20,8,256]{2,1,0:T(8,128)S(1)}, u32[]{:S(2)}, u32[]{:S(2)}) collective-permute-start(f32[20,8,256]{2,1,0:T(8,128)} %get-tuple-element.146), channel_id=1, source_target_pairs={{0,11},{1,10},{2,9},{3,8},{4,15},{5,14},{6,13},{7,12},{8,3},{9,2},... | collective-permute-start | bytes 491528 | tf_op jit(solution)/shard_map/ppermute | solution.py:43
  122.5 32.0 %collective-permute-start.26 = (f32[20,8,256]{2,1,0:T(8,128)}, f32[20,8,256]{2,1,0:T(8,128)S(1)}, u32[]{:S(2)}, u32[]{:S(2)}) collective-permute-start(f32[20,8,256]{2,1,0:T(8,128)} %get-tuple-element.147), channel_id=1, source_target_pairs={{0,10},{1,11},{2,8},{3,9},{4,14},{5,15},{6,12},{7,13},{8,2},{9,3},... | collective-permute-start | bytes 491528 | tf_op jit(solution)/shard_map/ppermute | solution.py:43
  133.2 168.6 %collective-permute-start = (f32[128,4,1024]{2,1,0:T(4,128)}, f32[128,4,1024]{2,1,0:T(4,128)}, u32[]{:S(2)}, u32[]{:S(2)}) collective-permute-start(f32[128,4,1024]{2,1,0:T(4,128)} %get-tuple-element.115), channel_id=1, source_target_pairs={{1,0},{2,1},{3,2},{4,3},{5,4},{6,5},{7,6},{8,7},{9,8},{10,9},{11,1... | collective-permute-start | bytes 6291464 | tf_op jit(solution)/shard_map/ppermute | solution.py:316
  144.0 38.4 %collective-permute-start.27 = (f32[20,8,256]{2,1,0:T(8,128)}, f32[20,8,256]{2,1,0:T(8,128)S(1)}, u32[]{:S(2)}, u32[]{:S(2)}) collective-permute-start(f32[20,8,256]{2,1,0:T(8,128)} %get-tuple-element.148), channel_id=1, source_target_pairs={{0,9},{1,8},{2,11},{3,10},{4,13},{5,12},{6,15},{7,14},{8,1},{9,0},... | collective-permute-start | bytes 491528 | tf_op jit(solution)/shard_map/ppermute | solution.py:43
  154.5 27.9 %collective-permute-start.28 = (f32[20,8,256]{2,1,0:T(8,128)}, f32[20,8,256]{2,1,0:T(8,128)S(1)}, u32[]{:S(2)}, u32[]{:S(2)}) collective-permute-start(f32[20,8,256]{2,1,0:T(8,128)} %get-tuple-element.149), channel_id=1, source_target_pairs={{0,8},{1,9},{2,10},{3,11},{4,12},{5,13},{6,14},{7,15},{8,0},{9,1},... | collective-permute-start | bytes 491528 | tf_op jit(solution)/shard_map/ppermute | solution.py:43
  207.6 24.8 %collective-permute-start.11 = (f32[20,8,256]{2,1,0:T(8,128)}, f32[20,8,256]{2,1,0:T(8,128)}, u32[]{:S(2)}, u32[]{:S(2)}) collective-permute-start(f32[20,8,256]{2,1,0:T(8,128)} %get-tuple-element.132), channel_id=1, source_target_pairs={{0,10},{1,11},{2,8},{3,9},{4,14},{5,15},{6,12},{7,13},{8,2},{9,3},... | collective-permute-start | bytes 491528 | tf_op jit(solution)/shard_map/ppermute | solution.py:43
  232.5 24.0 %collective-permute-start.13 = (f32[20,8,256]{2,1,0:T(8,128)}, f32[20,8,256]{2,1,0:T(8,128)S(1)}, u32[]{:S(2)}, u32[]{:S(2)}) collective-permute-start(f32[20,8,256]{2,1,0:T(8,128)} %get-tuple-element.134), channel_id=1, source_target_pairs={{0,8},{1,9},{2,10},{3,11},{4,12},{5,13},{6,14},{7,15},{8,0},{9,1},... | collective-permute-start | bytes 491528 | tf_op jit(solution)/shard_map/ppermute | solution.py:43
  235.8 22.0 %collective-permute-start.14 = (f32[20,8,256]{2,1,0:T(8,128)}, f32[20,8,256]{2,1,0:T(8,128)S(1)}, u32[]{:S(2)}, u32[]{:S(2)}) collective-permute-start(f32[20,8,256]{2,1,0:T(8,128)} %get-tuple-element.135), channel_id=1, source_target_pairs={{0,7},{1,6},{2,5},{3,4},{4,3},{5,2},{6,1},{7,0},{8,15},{9,14},{10,... | collective-permute-start | bytes 491528 | tf_op jit(solution)/shard_map/ppermute | solution.py:43
  235.8 22.1 %collective-permute-start.15 = (f32[20,8,256]{2,1,0:T(8,128)}, f32[20,8,256]{2,1,0:T(8,128)S(1)}, u32[]{:S(2)}, u32[]{:S(2)}) collective-permute-start(f32[20,8,256]{2,1,0:T(8,128)} %get-tuple-element.136), channel_id=1, source_target_pairs={{0,6},{1,7},{2,4},{3,5},{4,2},{5,3},{6,0},{7,1},{8,14},{9,15},{10,... | collective-permute-start | bytes 491528 | tf_op jit(solution)/shard_map/ppermute | solution.py:43
  256.5 189.5 %collective-permute-start.5 = (f32[128,8,512]{2,1,0:T(8,128)}, f32[128,8,512]{2,1,0:T(8,128)}, u32[]{:S(2)}, u32[]{:S(2)}) collective-permute-start(f32[128,8,512]{2,1,0:T(8,128)} %get-tuple-element.126), channel_id=1, source_target_pairs={{0,16},{16,0},{1,17},{17,1},{2,18},{18,2},{3,19},{19,3},{4,20},{20... | collective-permute-start | bytes 6291464 | tf_op jit(solution)/shard_map/ppermute | solution.py:43
  277.1 17.2 %collective-permute-start.7 = (f32[20,8,256]{2,1,0:T(8,128)}, f32[20,8,256]{2,1,0:T(8,128)S(1)}, u32[]{:S(2)}, u32[]{:S(2)}) collective-permute-start(f32[20,8,256]{2,1,0:T(8,128)} %get-tuple-element.128), channel_id=1, source_target_pairs={{0,14},{1,15},{2,12},{3,13},{4,10},{5,11},{6,8},{7,9},{8,6},{9,7},... | collective-permute-start | bytes 491528 | tf_op jit(solution)/shard_map/ppermute | solution.py:43
  296.2 45.4 %collective-permute-start.53 = (f32[20,8,512]{2,1,0:T(8,128)}, f32[20,8,512]{2,1,0:T(8,128)S(1)}, u32[]{:S(2)}, u32[]{:S(2)}) collective-permute-start(f32[20,8,512]{2,1,0:T(8,128)} %get-tuple-element.176), channel_id=1, source_target_pairs={{0,14},{1,15},{2,12},{3,13},{4,10},{5,11},{6,8},{7,9},{8,6},{9,7},... | collective-permute-start | bytes 983048 | tf_op jit(solution)/shard_map/ppermute | solution.py:43
  299.9 55.2 %collective-permute-start.54 = (f32[20,8,512]{2,1,0:T(8,128)}, f32[20,8,512]{2,1,0:T(8,128)S(1)}, u32[]{:S(2)}, u32[]{:S(2)}) collective-permute-start(f32[20,8,512]{2,1,0:T(8,128)} %get-tuple-element.177), channel_id=1, source_target_pairs={{0,13},{1,12},{2,15},{3,14},{4,9},{5,8},{6,11},{7,10},{8,5},{9,4},... | collective-permute-start | bytes 983048 | tf_op jit(solution)/shard_map/ppermute | solution.py:43
  301.8 67.0 %collective-permute-start.55 = (f32[20,8,512]{2,1,0:T(8,128)}, f32[20,8,512]{2,1,0:T(8,128)S(1)}, u32[]{:S(2)}, u32[]{:S(2)}) collective-permute-start(f32[20,8,512]{2,1,0:T(8,128)} %get-tuple-element.178), channel_id=1, source_target_pairs={{0,12},{1,13},{2,14},{3,15},{4,8},{5,9},{6,10},{7,11},{8,4},{9,5},... | collective-permute-start | bytes 983048 | tf_op jit(solution)/shard_map/ppermute | solution.py:43
  307.5 92.7 %collective-permute-start.56 = (f32[20,8,512]{2,1,0:T(8,128)}, f32[20,8,512]{2,1,0:T(8,128)S(1)}, u32[]{:S(2)}, u32[]{:S(2)}) collective-permute-start(f32[20,8,512]{2,1,0:T(8,128)} %get-tuple-element.179), channel_id=1, source_target_pairs={{0,11},{1,10},{2,9},{3,8},{4,15},{5,14},{6,13},{7,12},{8,3},{9,2},... | collective-permute-start | bytes 983048 | tf_op jit(solution)/shard_map/ppermute | solution.py:43
  341.7 61.8 %collective-permute-start.57 = (f32[20,8,512]{2,1,0:T(8,128)}, f32[20,8,512]{2,1,0:T(8,128)S(1)}, u32[]{:S(2)}, u32[]{:S(2)}) collective-permute-start(f32[20,8,512]{2,1,0:T(8,128)} %get-tuple-element.180), channel_id=1, source_target_pairs={{0,10},{1,11},{2,8},{3,9},{4,14},{5,15},{6,12},{7,13},{8,2},{9,3},... | collective-permute-start | bytes 983048 | tf_op jit(solution)/shard_map/ppermute | solution.py:43
  355.1 54.5 %collective-permute-start.58 = (f32[20,8,512]{2,1,0:T(8,128)}, f32[20,8,512]{2,1,0:T(8,128)S(1)}, u32[]{:S(2)}, u32[]{:S(2)}) collective-permute-start(f32[20,8,512]{2,1,0:T(8,128)} %get-tuple-element.181), channel_id=1, source_target_pairs={{0,9},{1,8},{2,11},{3,10},{4,13},{5,12},{6,15},{7,14},{8,1},{9,0},... | collective-permute-start | bytes 983048 | tf_op jit(solution)/shard_map/ppermute | solution.py:43
  368.8 48.4 %collective-permute-start.59 = (f32[20,8,512]{2,1,0:T(8,128)}, f32[20,8,512]{2,1,0:T(8,128)}, u32[]{:S(2)}, u32[]{:S(2)}) collective-permute-start(f32[20,8,512]{2,1,0:T(8,128)} %get-tuple-element.182), channel_id=1, source_target_pairs={{0,8},{1,9},{2,10},{3,11},{4,12},{5,13},{6,14},{7,15},{8,0},{9,1},... | collective-permute-start | bytes 983048 | tf_op jit(solution)/shard_map/ppermute | solution.py:43
  400.2 61.1 %collective-permute-start.82 = (f32[128,8,256]{2,1,0:T(8,128)}, f32[128,8,256]{2,1,0:T(8,128)S(1)}, u32[]{:S(2)}, u32[]{:S(2)}) collective-permute-start(f32[128,8,256]{2,1,0:T(8,128)} %get-tuple-element.208), channel_id=1, source_target_pairs={{0,16},{16,0},{1,17},{17,1},{2,18},{18,2},{3,19},{19,3},{4,20},{20... | collective-permute-start | bytes 3145736 | tf_op jit(solution)/shard_map/ppermute | solution.py:43
  403.4 21.1 %collective-permute-start.60 = (f32[20,8,512]{2,1,0:T(8,128)}, f32[20,8,512]{2,1,0:T(8,128)S(1)}, u32[]{:S(2)}, u32[]{:S(2)}) collective-permute-start(f32[20,8,512]{2,1,0:T(8,128)} %get-tuple-element.183), channel_id=1, source_target_pairs={{0,7},{1,6},{2,5},{3,4},{4,3},{5,2},{6,1},{7,0},{8,15},{9,14},{10,... | collective-permute-start | bytes 983048 | tf_op jit(solution)/shard_map/ppermute | solution.py:43
  409.7 21.8 %collective-permute-start.61 = (f32[20,8,512]{2,1,0:T(8,128)}, f32[20,8,512]{2,1,0:T(8,128)S(1)}, u32[]{:S(2)}, u32[]{:S(2)}) collective-permute-start(f32[20,8,512]{2,1,0:T(8,128)} %get-tuple-element.184), channel_id=1, source_target_pairs={{0,6},{1,7},{2,4},{3,5},{4,2},{5,3},{6,0},{7,1},{8,14},{9,15},{10,... | collective-permute-start | bytes 983048 | tf_op jit(solution)/shard_map/ppermute | solution.py:43
  417.2 57.5 %collective-permute-start.2 = (f32[128,8,256]{2,1,0:T(8,128)}, f32[128,8,256]{2,1,0:T(8,128)S(1)}, u32[]{:S(2)}, u32[]{:S(2)}) collective-permute-start(f32[128,8,256]{2,1,0:T(8,128)} %get-tuple-element.120), channel_id=1, source_target_pairs={{0,16},{16,0},{1,17},{17,1},{2,18},{18,2},{3,19},{19,3},{4,20},{20... | collective-permute-start | bytes 3145736 | tf_op jit(solution)/shard_map/ppermute | solution.py:43
  438.3 18.0 %collective-permute-start.64 = (f32[20,8,512]{2,1,0:T(8,128)}, f32[20,8,512]{2,1,0:T(8,128)}, u32[]{:S(2)}, u32[]{:S(2)}) collective-permute-start(f32[20,8,512]{2,1,0:T(8,128)} %get-tuple-element.187), channel_id=1, source_target_pairs={{0,3},{1,2},{2,1},{3,0},{4,7},{5,6},{6,5},{7,4},{8,11},{9,10},{10,... | collective-permute-start | bytes 983048 | tf_op jit(solution)/shard_map/ppermute | solution.py:43
  468.4 23.5 %collective-permute-start.84 = (f32[20,8,256]{2,1,0:T(8,128)}, f32[20,8,256]{2,1,0:T(8,128)S(1)}, u32[]{:S(2)}, u32[]{:S(2)}) collective-permute-start(f32[20,8,256]{2,1,0:T(8,128)} %get-tuple-element.210), channel_id=1, source_target_pairs={{0,14},{1,15},{2,12},{3,13},{4,10},{5,11},{6,8},{7,9},{8,6},{9,7},... | collective-permute-start | bytes 491528 | tf_op jit(solution)/shard_map/ppermute | solution.py:43
  470.8 24.8 %collective-permute-start.85 = (f32[20,8,256]{2,1,0:T(8,128)}, f32[20,8,256]{2,1,0:T(8,128)S(1)}, u32[]{:S(2)}, u32[]{:S(2)}) collective-permute-start(f32[20,8,256]{2,1,0:T(8,128)} %get-tuple-element.211), channel_id=1, source_target_pairs={{0,13},{1,12},{2,15},{3,14},{4,9},{5,8},{6,11},{7,10},{8,5},{9,4},... | collective-permute-start | bytes 491528 | tf_op jit(solution)/shard_map/ppermute | solution.py:43
  472.9 32.1 %collective-permute-start.86 = (f32[20,8,256]{2,1,0:T(8,128)}, f32[20,8,256]{2,1,0:T(8,128)S(1)}, u32[]{:S(2)}, u32[]{:S(2)}) collective-permute-start(f32[20,8,256]{2,1,0:T(8,128)} %get-tuple-element.212), channel_id=1, source_target_pairs={{0,12},{1,13},{2,14},{3,15},{4,8},{5,9},{6,10},{7,11},{8,4},{9,5},... | collective-permute-start | bytes 491528 | tf_op jit(solution)/shard_map/ppermute | solution.py:43
  474.7 40.9 %collective-permute-start.87 = (f32[20,8,256]{2,1,0:T(8,128)}, f32[20,8,256]{2,1,0:T(8,128)S(1)}, u32[]{:S(2)}, u32[]{:S(2)}) collective-permute-start(f32[20,8,256]{2,1,0:T(8,128)} %get-tuple-element.213), channel_id=1, source_target_pairs={{0,11},{1,10},{2,9},{3,8},{4,15},{5,14},{6,13},{7,12},{8,3},{9,2},... | collective-permute-start | bytes 491528 | tf_op jit(solution)/shard_map/ppermute | solution.py:43
  476.2 41.8 %collective-permute-start.88 = (f32[20,8,256]{2,1,0:T(8,128)}, f32[20,8,256]{2,1,0:T(8,128)S(1)}, u32[]{:S(2)}, u32[]{:S(2)}) collective-permute-start(f32[20,8,256]{2,1,0:T(8,128)} %get-tuple-element.214), channel_id=1, source_target_pairs={{0,10},{1,11},{2,8},{3,9},{4,14},{5,15},{6,12},{7,13},{8,2},{9,3},... | collective-permute-start | bytes 491528 | tf_op jit(solution)/shard_map/ppermute | solution.py:43
  491.8 30.5 %collective-permute-start.89 = (f32[20,8,256]{2,1,0:T(8,128)}, f32[20,8,256]{2,1,0:T(8,128)S(1)}, u32[]{:S(2)}, u32[]{:S(2)}) collective-permute-start(f32[20,8,256]{2,1,0:T(8,128)} %get-tuple-element.215), channel_id=1, source_target_pairs={{0,9},{1,8},{2,11},{3,10},{4,13},{5,12},{6,15},{7,14},{8,1},{9,0},... | collective-permute-start | bytes 491528 | tf_op jit(solution)/shard_map/ppermute | solution.py:43
  495.6 43.2 %collective-permute-start.90 = (f32[20,8,256]{2,1,0:T(8,128)}, f32[20,8,256]{2,1,0:T(8,128)S(1)}, u32[]{:S(2)}, u32[]{:S(2)}) collective-permute-start(f32[20,8,256]{2,1,0:T(8,128)} %get-tuple-element.216), channel_id=1, source_target_pairs={{0,8},{1,9},{2,10},{3,11},{4,12},{5,13},{6,14},{7,15},{8,0},{9,1},... | collective-permute-start | bytes 491528 | tf_op jit(solution)/shard_map/ppermute | solution.py:43
  505.0 37.9 %collective-permute-start.91 = (f32[20,8,256]{2,1,0:T(8,128)}, f32[20,8,256]{2,1,0:T(8,128)S(1)}, u32[]{:S(2)}, u32[]{:S(2)}) collective-permute-start(f32[20,8,256]{2,1,0:T(8,128)} %get-tuple-element.217), channel_id=1, source_target_pairs={{0,7},{1,6},{2,5},{3,4},{4,3},{5,2},{6,1},{7,0},{8,15},{9,14},{10,... | collective-permute-start | bytes 491528 | tf_op jit(solution)/shard_map/ppermute | solution.py:43
  515.6 28.8 %collective-permute-start.92 = (f32[20,8,256]{2,1,0:T(8,128)}, f32[20,8,256]{2,1,0:T(8,128)S(1)}, u32[]{:S(2)}, u32[]{:S(2)}) collective-permute-start(f32[20,8,256]{2,1,0:T(8,128)} %get-tuple-element.218), channel_id=1, source_target_pairs={{0,6},{1,7},{2,4},{3,5},{4,2},{5,3},{6,0},{7,1},{8,14},{9,15},{10,... | collective-permute-start | bytes 491528 | tf_op jit(solution)/shard_map/ppermute | solution.py:43
  518.0 27.6 %collective-permute-start.36 = (f32[20,8,512]{2,1,0:T(8,128)S(1)}, f32[20,8,512]{2,1,0:T(8,128)S(1)}, u32[]{:S(2)}, u32[]{:S(2)}) collective-permute-start(f32[20,8,512]{2,1,0:T(8,128)S(1)} %copy-done.68), channel_id=1, source_target_pairs={{0,15},{1,14},{2,13},{3,12},{4,11},{5,10},{6,9},{7,8},{8,7},{9,6},... | collective-permute-start | bytes 983048 | tf_op jit(solution)/shard_map/ppermute | solution.py:43
  522.3 46.8 %collective-permute-start.37 = (f32[20,8,512]{2,1,0:T(8,128)S(1)}, f32[20,8,512]{2,1,0:T(8,128)S(1)}, u32[]{:S(2)}, u32[]{:S(2)}) collective-permute-start(f32[20,8,512]{2,1,0:T(8,128)S(1)} %copy-done.67), channel_id=1, source_target_pairs={{0,14},{1,15},{2,12},{3,13},{4,10},{5,11},{6,8},{7,9},{8,6},{9,7},... | collective-permute-start | bytes 983048 | tf_op jit(solution)/shard_map/ppermute | solution.py:43
  538.8 44.6 %collective-permute-start.38 = (f32[20,8,512]{2,1,0:T(8,128)}, f32[20,8,512]{2,1,0:T(8,128)S(1)}, u32[]{:S(2)}, u32[]{:S(2)}) collective-permute-start(f32[20,8,512]{2,1,0:T(8,128)} %get-tuple-element.159), channel_id=1, source_target_pairs={{0,13},{1,12},{2,15},{3,14},{4,9},{5,8},{6,11},{7,10},{8,5},{9,4},... | collective-permute-start | bytes 983048 | tf_op jit(solution)/shard_map/ppermute | solution.py:43
  543.5 52.8 %collective-permute-start.39 = (f32[20,8,512]{2,1,0:T(8,128)}, f32[20,8,512]{2,1,0:T(8,128)S(1)}, u32[]{:S(2)}, u32[]{:S(2)}) collective-permute-start(f32[20,8,512]{2,1,0:T(8,128)} %get-tuple-element.160), channel_id=1, source_target_pairs={{0,12},{1,13},{2,14},{3,15},{4,8},{5,9},{6,10},{7,11},{8,4},{9,5},... | collective-permute-start | bytes 983048 | tf_op jit(solution)/shard_map/ppermute | solution.py:43
  545.1 72.4 %collective-permute-start.40 = (f32[20,8,512]{2,1,0:T(8,128)}, f32[20,8,512]{2,1,0:T(8,128)S(1)}, u32[]{:S(2)}, u32[]{:S(2)}) collective-permute-start(f32[20,8,512]{2,1,0:T(8,128)} %get-tuple-element.161), channel_id=1, source_target_pairs={{0,11},{1,10},{2,9},{3,8},{4,15},{5,14},{6,13},{7,12},{8,3},{9,2},... | collective-permute-start | bytes 983048 | tf_op jit(solution)/shard_map/ppermute | solution.py:43
  545.6 77.8 %collective-permute-start.41 = (f32[20,8,512]{2,1,0:T(8,128)}, f32[20,8,512]{2,1,0:T(8,128)S(1)}, u32[]{:S(2)}, u32[]{:S(2)}) collective-permute-start(f32[20,8,512]{2,1,0:T(8,128)} %get-tuple-element.162), channel_id=1, source_target_pairs={{0,10},{1,11},{2,8},{3,9},{4,14},{5,15},{6,12},{7,13},{8,2},{9,3},... | collective-permute-start | bytes 983048 | tf_op jit(solution)/shard_map/ppermute | solution.py:43
  569.1 62.5 %collective-permute-start.42 = (f32[20,8,512]{2,1,0:T(8,128)}, f32[20,8,512]{2,1,0:T(8,128)S(1)}, u32[]{:S(2)}, u32[]{:S(2)}) collective-permute-start(f32[20,8,512]{2,1,0:T(8,128)} %get-tuple-element.163), channel_id=1, source_target_pairs={{0,9},{1,8},{2,11},{3,10},{4,13},{5,12},{6,15},{7,14},{8,1},{9,0},... | collective-permute-start | bytes 983048 | tf_op jit(solution)/shard_map/ppermute | solution.py:43
  583.4 53.8 %collective-permute-start.43 = (f32[20,8,512]{2,1,0:T(8,128)}, f32[20,8,512]{2,1,0:T(8,128)}, u32[]{:S(2)}, u32[]{:S(2)}) collective-permute-start(f32[20,8,512]{2,1,0:T(8,128)} %get-tuple-element.164), channel_id=1, source_target_pairs={{0,8},{1,9},{2,10},{3,11},{4,12},{5,13},{6,14},{7,15},{8,0},{9,1},... | collective-permute-start | bytes 983048 | tf_op jit(solution)/shard_map/ppermute | solution.py:43
  596.3 48.8 %collective-permute-start.44 = (f32[20,8,512]{2,1,0:T(8,128)}, f32[20,8,512]{2,1,0:T(8,128)}, u32[]{:S(2)}, u32[]{:S(2)}) collective-permute-start(f32[20,8,512]{2,1,0:T(8,128)} %get-tuple-element.165), channel_id=1, source_target_pairs={{0,7},{1,6},{2,5},{3,4},{4,3},{5,2},{6,1},{7,0},{8,15},{9,14},{10,... | collective-permute-start | bytes 983048 | tf_op jit(solution)/shard_map/ppermute | solution.py:43
  617.5 34.7 %collective-permute-start.45 = (f32[20,8,512]{2,1,0:T(8,128)}, f32[20,8,512]{2,1,0:T(8,128)}, u32[]{:S(2)}, u32[]{:S(2)}) collective-permute-start(f32[20,8,512]{2,1,0:T(8,128)} %get-tuple-element.166), channel_id=1, source_target_pairs={{0,6},{1,7},{2,4},{3,5},{4,2},{5,3},{6,0},{7,1},{8,14},{9,15},{10,... | collective-permute-start | bytes 983048 | tf_op jit(solution)/shard_map/ppermute | solution.py:43
  623.4 35.7 %collective-permute-start.46 = (f32[20,8,512]{2,1,0:T(8,128)}, f32[20,8,512]{2,1,0:T(8,128)}, u32[]{:S(2)}, u32[]{:S(2)}) collective-permute-start(f32[20,8,512]{2,1,0:T(8,128)} %get-tuple-element.167), channel_id=1, source_target_pairs={{0,5},{1,4},{2,7},{3,6},{4,1},{5,0},{6,3},{7,2},{8,13},{9,12},{10,... | collective-permute-start | bytes 983048 | tf_op jit(solution)/shard_map/ppermute | solution.py:43
  631.6 34.3 %collective-permute-start.47 = (f32[20,8,512]{2,1,0:T(8,128)}, f32[20,8,512]{2,1,0:T(8,128)}, u32[]{:S(2)}, u32[]{:S(2)}) collective-permute-start(f32[20,8,512]{2,1,0:T(8,128)} %get-tuple-element.168), channel_id=1, source_target_pairs={{0,4},{1,5},{2,6},{3,7},{4,0},{5,1},{6,2},{7,3},{8,12},{9,13},{10,... | collective-permute-start | bytes 983048 | tf_op jit(solution)/shard_map/ppermute | solution.py:43
  637.2 28.7 %collective-permute-start.48 = (f32[20,8,512]{2,1,0:T(8,128)}, f32[20,8,512]{2,1,0:T(8,128)}, u32[]{:S(2)}, u32[]{:S(2)}) collective-permute-start(f32[20,8,512]{2,1,0:T(8,128)} %get-tuple-element.169), channel_id=1, source_target_pairs={{0,3},{1,2},{2,1},{3,0},{4,7},{5,6},{6,5},{7,4},{8,11},{9,10},{10,... | collective-permute-start | bytes 983048 | tf_op jit(solution)/shard_map/ppermute | solution.py:43
  645.2 21.8 %collective-permute-start.49 = (f32[20,8,512]{2,1,0:T(8,128)}, f32[20,8,512]{2,1,0:T(8,128)}, u32[]{:S(2)}, u32[]{:S(2)}) collective-permute-start(f32[20,8,512]{2,1,0:T(8,128)} %get-tuple-element.170), channel_id=1, source_target_pairs={{0,2},{1,3},{2,0},{3,1},{4,6},{5,7},{6,4},{7,5},{8,10},{9,11},{10,... | collective-permute-start | bytes 983048 | tf_op jit(solution)/shard_map/ppermute | solution.py:43
  659.1 18.3 %collective-permute-start.93 = (f32[20,8,256]{2,1,0:T(8,128)}, f32[20,8,256]{2,1,0:T(8,128)}, u32[]{:S(2)}, u32[]{:S(2)}) collective-permute-start(f32[20,8,256]{2,1,0:T(8,128)} %get-tuple-element.219), channel_id=1, source_target_pairs={{0,5},{1,4},{2,7},{3,6},{4,1},{5,0},{6,3},{7,2},{8,13},{9,12},{10,... | collective-permute-start | bytes 491528 | tf_op jit(solution)/shard_map/ppermute | solution.py:43
  667.0 16.4 %collective-permute-start.96 = (f32[20,8,256]{2,1,0:T(8,128)}, f32[20,8,256]{2,1,0:T(8,128)}, u32[]{:S(2)}, u32[]{:S(2)}) collective-permute-start(f32[20,8,256]{2,1,0:T(8,128)} %get-tuple-element.222), channel_id=1, source_target_pairs={{0,2},{1,3},{2,0},{3,1},{4,6},{5,7},{6,4},{7,5},{8,10},{9,11},{10,... | collective-permute-start | bytes 491528 | tf_op jit(solution)/shard_map/ppermute | solution.py:43
  667.8 17.6 %collective-permute-start.97 = (f32[20,8,256]{2,1,0:T(8,128)}, f32[20,8,256]{2,1,0:T(8,128)}, u32[]{:S(2)}, u32[]{:S(2)}) collective-permute-start(f32[20,8,256]{2,1,0:T(8,128)} %get-tuple-element.223), channel_id=1, source_target_pairs={{0,1},{1,0},{2,3},{3,2},{4,5},{5,4},{6,7},{7,6},{8,9},{9,8},{10,11... | collective-permute-start | bytes 491528 | tf_op jit(solution)/shard_map/ppermute | solution.py:43
  679.4 25.4 %collective-permute-start.68 = (f32[20,8,256]{2,1,0:T(8,128)}, f32[20,8,256]{2,1,0:T(8,128)S(1)}, u32[]{:S(2)}, u32[]{:S(2)}) collective-permute-start(f32[20,8,256]{2,1,0:T(8,128)} %get-tuple-element.192), channel_id=1, source_target_pairs={{0,14},{1,15},{2,12},{3,13},{4,10},{5,11},{6,8},{7,9},{8,6},{9,7},... | collective-permute-start | bytes 491528 | tf_op jit(solution)/shard_map/ppermute | solution.py:43
  681.8 26.5 %collective-permute-start.69 = (f32[20,8,256]{2,1,0:T(8,128)}, f32[20,8,256]{2,1,0:T(8,128)S(1)}, u32[]{:S(2)}, u32[]{:S(2)}) collective-permute-start(f32[20,8,256]{2,1,0:T(8,128)} %get-tuple-element.193), channel_id=1, source_target_pairs={{0,13},{1,12},{2,15},{3,14},{4,9},{5,8},{6,11},{7,10},{8,5},{9,4},... | collective-permute-start | bytes 491528 | tf_op jit(solution)/shard_map/ppermute | solution.py:43
  683.4 34.5 %collective-permute-start.70 = (f32[20,8,256]{2,1,0:T(8,128)}, f32[20,8,256]{2,1,0:T(8,128)S(1)}, u32[]{:S(2)}, u32[]{:S(2)}) collective-permute-start(f32[20,8,256]{2,1,0:T(8,128)} %get-tuple-element.194), channel_id=1, source_target_pairs={{0,12},{1,13},{2,14},{3,15},{4,8},{5,9},{6,10},{7,11},{8,4},{9,5},... | collective-permute-start | bytes 491528 | tf_op jit(solution)/shard_map/ppermute | solution.py:43
  685.4 43.1 %collective-permute-start.71 = (f32[20,8,256]{2,1,0:T(8,128)}, f32[20,8,256]{2,1,0:T(8,128)S(1)}, u32[]{:S(2)}, u32[]{:S(2)}) collective-permute-start(f32[20,8,256]{2,1,0:T(8,128)} %get-tuple-element.195), channel_id=1, source_target_pairs={{0,11},{1,10},{2,9},{3,8},{4,15},{5,14},{6,13},{7,12},{8,3},{9,2},... | collective-permute-start | bytes 491528 | tf_op jit(solution)/shard_map/ppermute | solution.py:43
  687.0 45.0 %collective-permute-start.72 = (f32[20,8,256]{2,1,0:T(8,128)}, f32[20,8,256]{2,1,0:T(8,128)S(1)}, u32[]{:S(2)}, u32[]{:S(2)}) collective-permute-start(f32[20,8,256]{2,1,0:T(8,128)} %get-tuple-element.196), channel_id=1, source_target_pairs={{0,10},{1,11},{2,8},{3,9},{4,14},{5,15},{6,12},{7,13},{8,2},{9,3},... | collective-permute-start | bytes 491528 | tf_op jit(solution)/shard_map/ppermute | solution.py:43
  704.7 30.5 %collective-permute-start.73 = (f32[20,8,256]{2,1,0:T(8,128)}, f32[20,8,256]{2,1,0:T(8,128)S(1)}, u32[]{:S(2)}, u32[]{:S(2)}) collective-permute-start(f32[20,8,256]{2,1,0:T(8,128)} %get-tuple-element.197), channel_id=1, source_target_pairs={{0,9},{1,8},{2,11},{3,10},{4,13},{5,12},{6,15},{7,14},{8,1},{9,0},... | collective-permute-start | bytes 491528 | tf_op jit(solution)/shard_map/ppermute | solution.py:43
  708.3 30.1 %collective-permute-start.74 = (f32[20,8,256]{2,1,0:T(8,128)}, f32[20,8,256]{2,1,0:T(8,128)S(1)}, u32[]{:S(2)}, u32[]{:S(2)}) collective-permute-start(f32[20,8,256]{2,1,0:T(8,128)} %get-tuple-element.198), channel_id=1, source_target_pairs={{0,8},{1,9},{2,10},{3,11},{4,12},{5,13},{6,14},{7,15},{8,0},{9,1},... | collective-permute-start | bytes 491528 | tf_op jit(solution)/shard_map/ppermute | solution.py:43
  717.9 23.1 %collective-permute-start.75 = (f32[20,8,256]{2,1,0:T(8,128)}, f32[20,8,256]{2,1,0:T(8,128)S(1)}, u32[]{:S(2)}, u32[]{:S(2)}) collective-permute-start(f32[20,8,256]{2,1,0:T(8,128)} %get-tuple-element.199), channel_id=1, source_target_pairs={{0,7},{1,6},{2,5},{3,4},{4,3},{5,2},{6,1},{7,0},{8,15},{9,14},{10,... | collective-permute-start | bytes 491528 | tf_op jit(solution)/shard_map/ppermute | solution.py:43
  731.9 16.2 %collective-permute-start.77 = (f32[20,8,256]{2,1,0:T(8,128)}, f32[20,8,256]{2,1,0:T(8,128)S(1)}, u32[]{:S(2)}, u32[]{:S(2)}) collective-permute-start(f32[20,8,256]{2,1,0:T(8,128)} %get-tuple-element.201), channel_id=1, source_target_pairs={{0,5},{1,4},{2,7},{3,6},{4,1},{5,0},{6,3},{7,2},{8,13},{9,12},{10,... | collective-permute-start | bytes 491528 | tf_op jit(solution)/shard_map/ppermute | solution.py:43
  (111 other events, 2963.6 us)

commit v2 on v1

--- a/solution.py
+++ b/solution.py
@@ -45,61 +45,95 @@
 
 def beam_kernel(above, below, first, last, count, col_width, pieces, waits, *refs):
     here_ref, taps_ref, prev_ref, cur_ref, next_ref, mprev_ref, mcur_ref, mnext_ref = refs[:8]
-    outs = refs[8 + waits : -2]
-    window, scratch = refs[-2:]
+    outs = refs[8 + waits : -3]
+    masks, window, scratch = refs[-3:]
     group = cur_ref.shape[0]
     tiles = cur_ref.shape[2] // LANES
     base = pl.program_id(0) * group
     edges = list(outs[count * len(pieces) :])
+    narrow = sorted(
+        (owner * col_width + col) // LANES + j
+        for owner in range(count)
+        for col, width in pieces
+        for j in range(width // LANES)
+    )
+    wide = sorted({b + j for b in narrow for j in (-1, 0, 1)} & set(range(tiles)))
     lane = lax.broadcasted_iota(jnp.int32, (ROWS, LANES), 1)
-    zeros = jnp.zeros((ROWS, LANES), jnp.float32)
-
-    def one(c, slot):
+
+    @pl.when(pl.program_id(0) == 0)
+    def _():
+        for j, ref in enumerate((mprev_ref, mcur_ref, mnext_ref)):
+            masks[j] = ref[...].astype(jnp.float32)
+
+    def along_rows(c, slot):
         taps = [taps_ref[(base + c) * (RMAX + 1) + k] for k in range(RMAX + 1)]
         sums = []
-        for b in range(tiles):
+        for b in wide if not edges else range(tiles):
             at = pl.ds(b * LANES, LANES)
+
+            def rows(start, size):
+                return pl.ds(2 * ((slot * tiles + b) * 3 * ROWS + start), size, stride=2)
+
             if above:
-                window[slot, b, ROWS - RMAX : ROWS] = prev_ref[c, :, at]
+                window[rows(ROWS - RMAX, RMAX)] = prev_ref[c, :, at]
             else:
-                prev = prev_ref[c, :, at] * mprev_ref[:, at].astype(jnp.float32)
-                window[slot, b, :ROWS] = prev
-            window[slot, b, ROWS : 2 * ROWS] = cur_ref[c, :, at] * mcur_ref[:, at].astype(jnp.float32)
+                prev = prev_ref[c, :, at] * masks[0, :, at]
+                window[rows(0, ROWS)] = prev
+                if first:
+                    edges[0][c, :, at] = prev[:RMAX]
+            cur = cur_ref[c, :, at] * masks[1, :, at]
+            window[rows(ROWS, ROWS)] = cur
             if below:
-                window[slot, b, 2 * ROWS : 2 * ROWS + RMAX] = next_ref[c, :, at]
+                window[rows(2 * ROWS, RMAX)] = next_ref[c, :, at]
             else:
-                after = next_ref[c, :, at] * mnext_ref[:, at].astype(jnp.float32)
-                window[slot, b, 2 * ROWS :] = after
-            total = taps[0] * window[slot, b, ROWS : 2 * ROWS]
+                after = next_ref[c, :, at] * masks[2, :, at]
+                window[rows(2 * ROWS, ROWS)] = after
+                if last:
+                    edges[-1][c, :, at] = after[ROWS - RMAX :]
+            total = taps[0] * cur
             for k in range(1, RMAX + 1):
                 total = total + taps[k] * (
-                    window[slot, b, ROWS - k : 2 * ROWS - k] + window[slot, b, ROWS + k : 2 * ROWS + k]
+                    window[rows(ROWS - k, ROWS)] + window[rows(ROWS + k, ROWS)]
                 )
             sums.append(total)
-            if first:
-                edges[0][c, :, at] = window[slot, b, :RMAX]
-            if last:
-                edges[-1][c, :, at] = window[slot, b, 3 * ROWS - RMAX :]
-        totals = [taps[0] * total for total in sums]
-        for k in range(1, RMAX + 1):
-            right = [pltpu.roll(total, k, 1) for total in sums]
-            left = [pltpu.roll(total, LANES - k, 1) for total in sums]
-            for b in range(tiles):
-                below_ = right[b - 1] if b else zeros
-                above_ = left[b + 1] if b + 1 < tiles else zeros
-                totals[b] = totals[b] + taps[k] * (
-                    jnp.where(lane < k, below_, right[b])
-                    + jnp.where(lane >= LANES - k, above_, left[b])
-                )
-        for b in range(tiles):
-            scratch[c, :, pl.ds(b * LANES, LANES)] = totals[b]
-
-    def pair(i, carry):
-        one(2 * i, 0)
-        one(2 * i + 1, 1)
-        return carry
-
-    lax.fori_loop(0, group // 2, pair, 0)
+        return sums
+
+    def along_cols(c, sums):
+        t = [taps_ref[(base + c) * (RMAX + 1) + k] for k in range(RMAX + 1)]
+        x = dict(zip(wide if not edges else range(tiles), sums))
+        right = {b: pltpu.roll(v, 1, 1) for b, v in x.items()}
+        left = {b: pltpu.roll(v, LANES - 1, 1) for b, v in x.items()}
+        low, high, middle = {}, {}, {}
+        for b in x:
+            before = jnp.where(lane < 1, right.get(b - 1, 0.0), right[b])
+            after = jnp.where(lane >= LANES - 1, left.get(b + 1, 0.0), left[b])
+            if b in narrow or b + 1 in narrow:
+                low[b] = t[4] * before + t[3] * x[b] + t[2] * after
+            if b in narrow:
+                middle[b] = t[1] * (before + after) + t[0] * x[b]
+            if b in narrow or b - 1 in narrow:
+                high[b] = t[2] * before + t[3] * x[b] + t[4] * after
+        if 0 in narrow:
+            low[-1] = jnp.where(lane >= LANES - 1, t[2] * left[0], 0.0)
+        if tiles - 1 in narrow:
+            high[tiles] = jnp.where(lane < 1, t[2] * right[tiles - 1], 0.0)
+        low = {b: pltpu.roll(v, 3, 1) for b, v in low.items()}
+        high = {b: pltpu.roll(v, LANES - 3, 1) for b, v in high.items()}
+        for b in narrow:
+            before = jnp.where(lane < 3, low[b - 1], low[b])
+            after = jnp.where(lane >= LANES - 3, high[b + 1], high[b])
+            scratch[c, :, pl.ds(b * LANES, LANES)] = middle[b] + (before + after)
+
+    def step(i, sums):
+        following = along_rows(2 * i + 2, 0), along_rows(2 * i + 3, 1)
+        along_cols(2 * i, sums[0])
+        along_cols(2 * i + 1, sums[1])
+        return following
+
+    start = along_rows(0, 0), along_rows(1, 1)
+    sums = lax.fori_loop(0, group // 2 - 1, step, start)
+    along_cols(group - 2, sums[0])
+    along_cols(group - 1, sums[1])
     me = here_ref[0]
     at = 0
     for step in range(count):
@@ -109,11 +143,11 @@
             at += 1
 
 
-def beam_block(sky, mask, up, down, taps, me, block, count, pieces, after):
+def beam_block(sky, mask, up, down, taps, me, block, count, pieces, edges, after):
     chans, rows, cols = sky.shape
     blocks = rows // ROWS
     above, below = block == 0, block == blocks - 1
-    first, last = block == 1 and blocks > 2, block == blocks - 2 and blocks > 2
+    first, last = edges and block == 1 and blocks > 2, edges and block == blocks - 2 and blocks > 2
     group = min(chans, 16)
     col_width = cols // count
     full = lambda b: pl.BlockSpec((group, ROWS, cols), lambda i: (i, b, 0))
@@ -148,7 +182,8 @@
         out_specs=out_specs,
         out_shape=out_shapes,
         scratch_shapes=[
-            pltpu.VMEM((2, cols // LANES, 3 * ROWS, LANES), jnp.float32),
+            pltpu.VMEM((3, ROWS, cols), jnp.float32),
+            pltpu.VMEM((2 * cols // LANES * 6 * ROWS, LANES), jnp.float32),
             pltpu.VMEM((group, ROWS, cols), jnp.float32),
         ],
         cost_estimate=LIGHT,
@@ -306,19 +341,23 @@
         edges["first"] = sky_cube[:, :RMAX] * mask[:, :RMAX]
         edges["last"] = sky_cube[:, rows - RMAX :] * mask[:, rows - RMAX :]
     up = down = result = None
+    calls = [
+        (block, fine if block in (order[0], order[-1]) else whole, True) for block in order
+    ]
     mixed, placed = [], []
-    for at, block in enumerate(order):
-        pieces = fine if at in (0, len(order) - 1) else whole
-        after = mixed[at - 2 : at - 1] if at >= 2 else []
+    for at, (block, pieces, sides) in enumerate(calls):
+        after = mixed[:1] if at >= 2 else []
         if block == 0 and up is None:
             up = lax.ppermute(edges["last"], "tile", forward)
         if block == blocks - 1 and down is None:
             down = lax.ppermute(edges["first"], "tile", backward)
-        cut = beam_block(sky_cube, pixel_mask, up, down, taps, here_chan, block, nchan, pieces, after)
+        cut = beam_block(
+            sky_cube, pixel_mask, up, down, taps, here_chan, block, nchan, pieces, sides, after
+        )
         extra = list(cut[nchan * len(pieces) :])
-        if blocks > 2 and block == 1:
+        if extra and block == 1:
             edges["first"] = extra[0]
-        if blocks > 2 and block == blocks - 2:
+        if extra and block == blocks - 2:
             edges["last"] = extra[-1]
         for j, (col, _) in enumerate(pieces):
             parts = [cut[j]]

time: 756 us -> 753 us (level)
  transfers between devices with their start and end apart: 98 -> 98, of which waited for: 47 -> 47; matrix products, arithmetic and copies ran while one was open for 0% -> 0% of each run, Pallas kernels for 14% -> 13%
where the time goes in v2:
time: 753 us; the launch traced here: 752 us
  starting transfers between devices  312 us (41%)
  waiting for transfers between devices  309 us (41%)
  Pallas kernels  120 us (16%)
    ppermute x96, waiting for transfers between devices, shift(): lax.ppermute(block, axis, [(i, partner(i, step, count)) for i in range(co...  309 us
    ppermute x96, starting transfers between devices, shift(): lax.ppermute(block, axis, [(i, partner(i, step, count)) for i in range(co...  303 us
    pallas_call x4, Pallas kernels, beam_block(): pl.pallas_call(lambda *refs: beam_kernel(above, below, first, last, count...  67.8 us
    pallas_call x6, Pallas kernels, mix(): pl.pallas_call(lambda *refs: mix_kernel(count, owners, len(after), *refs)...  31.2 us
    pallas_call x6, Pallas kernels, place(): pl.pallas_call(lambda *refs: place_kernel(owners, rows, block, col, width...  21.1 us
  transfers between devices with their start and end apart: 98, of which 47 were waited for; matrix products, arithmetic and copies ran while one was open for 0% of the time, Pallas kernels for 13%

profile of v2, /device:TPU:1, one launch (start us, length us, event | category | flops | bytes accessed | tf_op | source)
XLA Modules:
  0.0 751.8 jit_solution(17359768538617874169)
XLA Ops:
  1.9 17.0 %beam.4 = (f32[128,8,256]{2,1,0:T(8,128)}, f32[128,8,256]{2,1,0:T(8,128)}, f32[128,8,256]{2,1,0:T(8,128)}, f32[128,8,256]{2,1,0:T(8,128)}, f32[128,4,1024]{2,1,0:T(4,128)}) custom-call(s32[1]{0:T(128)} %bitcast.20.refs_0_, f32[640]{0:T(1024)} %reshape.75.refs_1_, f32[128,32,1024]{2,1,0:T(8,128)} %refs_4_.5, f32[128,32,1024]{2,1,0:T(8,128)} %refs_4_.5, ...), custom_call_target="tpu_custom_call" | custom-call | flops 1 | bytes 1 | tf_op jit(solution)/shard_map/beam/pallas_call | solution.py:166
  21.0 16.6 %beam.6 = (f32[128,8,512]{2,1,0:T(8,128)}, f32[128,8,512]{2,1,0:T(8,128)}, f32[128,4,1024]{2,1,0:T(4,128)}) custom-call(s32[1]{0:T(128)} %bitcast.20.refs_0_, f32[640]{0:T(1024)} %reshape.75.refs_1_, f32[128,32,1024]{2,1,0:T(8,128)} %refs_4_.5, f32[128,32,1024]{2,1,0:T(8,128)} %refs_4_.5, f32[128,32,1024]{2,1,0:T(8,128)} %refs_4_.5, s32[32,1024]{1,0:T(8,128)} %refs_7_.7, ...), custom_call_target="tpu_custom_call" | custom-call | flops 1 | bytes 1 | tf_op jit(solution)/shard_map/beam/pallas_call | solution.py:166
  39.1 4.5 collective-permute-start.3
  47.7 4.3 mix.6
  52.0 4.2 collective-permute-start.21
  56.3 55.4 %collective-permute-done.5.refs_2_ = f32[128,8,256]{2,1,0:T(8,128)} collective-permute-done((f32[128,8,256]{2,1,0:T(8,128)}, f32[128,8,256]{2,1,0:T(8,128)}, u32[]{:S(2)}, u32[]{:S(2)}) %collective-permute-start.5) | collective-permute-done | bytes 1048608 | tf_op jit(solution)/shard_map/ppermute | solution.py:43
  111.6 4.7 collective-permute-start.23
  116.8 4.0 collective-permute-done.23.refs_3_
  120.8 10.7 %collective-permute-start.26 = (f32[20,8,256]{2,1,0:T(8,128)}, f32[20,8,256]{2,1,0:T(8,128)S(1)}, u32[]{:S(2)}, u32[]{:S(2)}) collective-permute-start(f32[20,8,256]{2,1,0:T(8,128)} %get-tuple-element.147), channel_id=1, source_target_pairs={{0,10},{1,11},{2,8},{3,9},{4,14},{5,15},{6,12},{7,13},{8,2},{9,3},... | collective-permute-start | bytes 491528 | tf_op jit(solution)/shard_map/ppermute | solution.py:43
  131.5 4.4 collective-permute-start
  136.0 6.4 collective-permute-done.25.refs_5_
  142.4 10.5 %collective-permute-done.26.refs_6_ = f32[20,8,256]{2,1,0:T(8,128)S(1)} collective-permute-done((f32[20,8,256]{2,1,0:T(8,128)}, f32[20,8,256]{2,1,0:T(8,128)S(1)}, u32[]{:S(2)}, u32[]{:S(2)}) %collective-permute-start.26) | collective-permute-done | bytes 163872 | tf_op jit(solution)/shard_map/ppermute | solution.py:43
  152.8 27.9 %collective-permute-done.27.refs_7_ = f32[20,8,256]{2,1,0:T(8,128)S(1)} collective-permute-done((f32[20,8,256]{2,1,0:T(8,128)}, f32[20,8,256]{2,1,0:T(8,128)S(1)}, u32[]{:S(2)}, u32[]{:S(2)}) %collective-permute-start.27) | collective-permute-done | bytes 163872 | tf_op jit(solution)/shard_map/ppermute | solution.py:43
  180.8 7.6 %collective-permute-done.29.refs_9_ = f32[20,8,256]{2,1,0:T(8,128)} collective-permute-done((f32[20,8,256]{2,1,0:T(8,128)}, f32[20,8,256]{2,1,0:T(8,128)}, u32[]{:S(2)}, u32[]{:S(2)}) %collective-permute-start.29) | collective-permute-done | bytes 163872 | tf_op jit(solution)/shard_map/ppermute | solution.py:43
  188.5 6.2 collective-permute-done.31.refs_11_
  195.3 6.2 collective-permute-done.33.refs_13_
  201.5 4.4 mix.7
  206.1 3.6 collective-permute-start.11
  209.7 10.6 %collective-permute-done.10.refs_5_ = f32[20,8,256]{2,1,0:T(8,128)} collective-permute-done((f32[20,8,256]{2,1,0:T(8,128)}, f32[20,8,256]{2,1,0:T(8,128)}, u32[]{:S(2)}, u32[]{:S(2)}) %collective-permute-start.10) | collective-permute-done | bytes 163872 | tf_op jit(solution)/shard_map/ppermute | solution.py:43
  220.3 10.5 %collective-permute-done.11.refs_6_ = f32[20,8,256]{2,1,0:T(8,128)} collective-permute-done((f32[20,8,256]{2,1,0:T(8,128)}, f32[20,8,256]{2,1,0:T(8,128)}, u32[]{:S(2)}, u32[]{:S(2)}) %collective-permute-start.11) | collective-permute-done | bytes 163872 | tf_op jit(solution)/shard_map/ppermute | solution.py:43
  236.8 16.9 %beam.7 = (f32[128,8,512]{2,1,0:T(8,128)}, f32[128,8,512]{2,1,0:T(8,128)}) custom-call(s32[1]{0:T(128)} %bitcast.20.refs_0_, f32[640]{0:T(1024)} %reshape.75.refs_1_, f32[128,4,1024]{2,1,0:T(4,128)} %collective-permute-done.3.refs_2_, f32[128,32,1024]{2,1,0:T(8,128)} %refs_4_.5, f32[128,32,1024]{2,1,0:T(8,128)} %refs_4_.5, s32[32,1024]{1,0:T(8,128)} %refs_7_.7, ...), custom_call_target="tpu_custom_call" | custom-call | flops 1 | bytes 1 | tf_op jit(solution)/shard_map/beam/pallas_call | solution.py:166
  257.2 4.8 collective-permute-done.16.refs_11_
  274.4 5.1 collective-permute-start.7
  280.8 3.9 collective-permute-start.9
  284.7 6.9 mix.9
  301.1 3.7 collective-permute-done.52.refs_1_
  304.8 34.2 %collective-permute-start.56 = (f32[20,8,512]{2,1,0:T(8,128)}, f32[20,8,512]{2,1,0:T(8,128)S(1)}, u32[]{:S(2)}, u32[]{:S(2)}) collective-permute-start(f32[20,8,512]{2,1,0:T(8,128)} %get-tuple-element.179), channel_id=1, source_target_pairs={{0,11},{1,10},{2,9},{3,8},{4,15},{5,14},{6,13},{7,12},{8,3},{9,2},... | collective-permute-start | bytes 983048 | tf_op jit(solution)/shard_map/ppermute | solution.py:43
  338.9 13.5 %collective-permute-start.57 = (f32[20,8,512]{2,1,0:T(8,128)}, f32[20,8,512]{2,1,0:T(8,128)S(1)}, u32[]{:S(2)}, u32[]{:S(2)}) collective-permute-start(f32[20,8,512]{2,1,0:T(8,128)} %get-tuple-element.180), channel_id=1, source_target_pairs={{0,10},{1,11},{2,8},{3,9},{4,14},{5,15},{6,12},{7,13},{8,2},{9,3},... | collective-permute-start | bytes 983048 | tf_op jit(solution)/shard_map/ppermute | solution.py:43
  352.4 13.7 %collective-permute-start.58 = (f32[20,8,512]{2,1,0:T(8,128)}, f32[20,8,512]{2,1,0:T(8,128)S(1)}, u32[]{:S(2)}, u32[]{:S(2)}) collective-permute-start(f32[20,8,512]{2,1,0:T(8,128)} %get-tuple-element.181), channel_id=1, source_target_pairs={{0,9},{1,8},{2,11},{3,10},{4,13},{5,12},{6,15},{7,14},{8,1},{9,0},... | collective-permute-start | bytes 983048 | tf_op jit(solution)/shard_map/ppermute | solution.py:43
  366.1 13.5 %collective-permute-start.59 = (f32[20,8,512]{2,1,0:T(8,128)}, f32[20,8,512]{2,1,0:T(8,128)}, u32[]{:S(2)}, u32[]{:S(2)}) collective-permute-start(f32[20,8,512]{2,1,0:T(8,128)} %get-tuple-element.182), channel_id=1, source_target_pairs={{0,8},{1,9},{2,10},{3,11},{4,12},{5,13},{6,14},{7,15},{8,0},{9,1},... | collective-permute-start | bytes 983048 | tf_op jit(solution)/shard_map/ppermute | solution.py:43
  379.6 17.3 %beam.5 = (f32[128,8,256]{2,1,0:T(8,128)}, f32[128,8,256]{2,1,0:T(8,128)}, f32[128,8,256]{2,1,0:T(8,128)}, f32[128,8,256]{2,1,0:T(8,128)}) custom-call(s32[1]{0:T(128)} %bitcast.20.refs_0_, f32[640]{0:T(1024)} %reshape.75.refs_1_, f32[128,32,1024]{2,1,0:T(8,128)} %refs_4_.5, f32[128,32,1024]{2,1,0:T(8,128)} %refs_4_.5, ...), custom_call_target="tpu_custom_call" | custom-call | flops 1 | bytes 1 | tf_op jit(solution)/shard_map/beam/pallas_call | solution.py:166
  400.7 6.2 collective-permute-done.58.refs_7_
  406.9 7.6 %collective-permute-done.59.refs_8_ = f32[20,8,512]{2,1,0:T(8,128)} collective-permute-done((f32[20,8,512]{2,1,0:T(8,128)}, f32[20,8,512]{2,1,0:T(8,128)}, u32[]{:S(2)}, u32[]{:S(2)}) %collective-permute-start.59) | collective-permute-done | bytes 327712 | tf_op jit(solution)/shard_map/ppermute | solution.py:43
  414.8 6.9 collective-permute-done.60.refs_9_
  421.8 7.0 collective-permute-done.61.refs_10_
  428.8 6.8 collective-permute-done.62.refs_11_
  436.4 6.2 collective-permute-done.63.refs_12_
  446.7 6.9 mix.8
  453.7 4.9 place.8.refs_17_.refs_3_
  459.6 4.3 mix.11
  473.5 15.6 %collective-permute-start.88 = (f32[20,8,256]{2,1,0:T(8,128)}, f32[20,8,256]{2,1,0:T(8,128)S(1)}, u32[]{:S(2)}, u32[]{:S(2)}) collective-permute-start(f32[20,8,256]{2,1,0:T(8,128)} %get-tuple-element.214), channel_id=1, source_target_pairs={{0,10},{1,11},{2,8},{3,9},{4,14},{5,15},{6,12},{7,13},{8,2},{9,3},... | collective-permute-start | bytes 491528 | tf_op jit(solution)/shard_map/ppermute | solution.py:43
  489.1 3.7 collective-permute-start.89
  492.9 9.4 %collective-permute-start.90 = (f32[20,8,256]{2,1,0:T(8,128)}, f32[20,8,256]{2,1,0:T(8,128)S(1)}, u32[]{:S(2)}, u32[]{:S(2)}) collective-permute-start(f32[20,8,256]{2,1,0:T(8,128)} %get-tuple-element.216), channel_id=1, source_target_pairs={{0,8},{1,9},{2,10},{3,11},{4,12},{5,13},{6,14},{7,15},{8,0},{9,1},... | collective-permute-start | bytes 491528 | tf_op jit(solution)/shard_map/ppermute | solution.py:43
  502.3 7.8 %collective-permute-start.91 = (f32[20,8,256]{2,1,0:T(8,128)}, f32[20,8,256]{2,1,0:T(8,128)S(1)}, u32[]{:S(2)}, u32[]{:S(2)}) collective-permute-start(f32[20,8,256]{2,1,0:T(8,128)} %get-tuple-element.217), channel_id=1, source_target_pairs={{0,7},{1,6},{2,5},{3,4},{4,3},{5,2},{6,1},{7,0},{8,15},{9,14},{10,... | collective-permute-start | bytes 491528 | tf_op jit(solution)/shard_map/ppermute | solution.py:43
  515.3 3.5 collective-permute-start.36
  521.5 14.6 %collective-permute-done.90.refs_8_ = f32[20,8,256]{2,1,0:T(8,128)S(1)} collective-permute-done((f32[20,8,256]{2,1,0:T(8,128)}, f32[20,8,256]{2,1,0:T(8,128)S(1)}, u32[]{:S(2)}, u32[]{:S(2)}) %collective-permute-start.90) | collective-permute-done | bytes 163872 | tf_op jit(solution)/shard_map/ppermute | solution.py:43
  542.9 23.5 %collective-permute-start.41 = (f32[20,8,512]{2,1,0:T(8,128)}, f32[20,8,512]{2,1,0:T(8,128)S(1)}, u32[]{:S(2)}, u32[]{:S(2)}) collective-permute-start(f32[20,8,512]{2,1,0:T(8,128)} %get-tuple-element.162), channel_id=1, source_target_pairs={{0,10},{1,11},{2,8},{3,9},{4,14},{5,15},{6,12},{7,13},{8,2},{9,3},... | collective-permute-start | bytes 983048 | tf_op jit(solution)/shard_map/ppermute | solution.py:43
  566.4 14.3 %collective-permute-start.42 = (f32[20,8,512]{2,1,0:T(8,128)}, f32[20,8,512]{2,1,0:T(8,128)S(1)}, u32[]{:S(2)}, u32[]{:S(2)}) collective-permute-start(f32[20,8,512]{2,1,0:T(8,128)} %get-tuple-element.163), channel_id=1, source_target_pairs={{0,9},{1,8},{2,11},{3,10},{4,13},{5,12},{6,15},{7,14},{8,1},{9,0},... | collective-permute-start | bytes 983048 | tf_op jit(solution)/shard_map/ppermute | solution.py:43
  580.7 12.9 %collective-permute-start.43 = (f32[20,8,512]{2,1,0:T(8,128)}, f32[20,8,512]{2,1,0:T(8,128)}, u32[]{:S(2)}, u32[]{:S(2)}) collective-permute-start(f32[20,8,512]{2,1,0:T(8,128)} %get-tuple-element.164), channel_id=1, source_target_pairs={{0,8},{1,9},{2,10},{3,11},{4,12},{5,13},{6,14},{7,15},{8,0},{9,1},... | collective-permute-start | bytes 983048 | tf_op jit(solution)/shard_map/ppermute | solution.py:43
  593.6 14.9 %collective-permute-start.44 = (f32[20,8,512]{2,1,0:T(8,128)}, f32[20,8,512]{2,1,0:T(8,128)}, u32[]{:S(2)}, u32[]{:S(2)}) collective-permute-start(f32[20,8,512]{2,1,0:T(8,128)} %get-tuple-element.165), channel_id=1, source_target_pairs={{0,7},{1,6},{2,5},{3,4},{4,3},{5,2},{6,1},{7,0},{8,15},{9,14},{10,... | collective-permute-start | bytes 983048 | tf_op jit(solution)/shard_map/ppermute | solution.py:43
  608.5 6.3 collective-permute-done.40.refs_5_
  614.8 5.9 collective-permute-done.41.refs_6_
  620.7 8.2 %collective-permute-done.42.refs_7_ = f32[20,8,512]{2,1,0:T(8,128)S(1)} collective-permute-done((f32[20,8,512]{2,1,0:T(8,128)}, f32[20,8,512]{2,1,0:T(8,128)S(1)}, u32[]{:S(2)}, u32[]{:S(2)}) %collective-permute-start.42) | collective-permute-done | bytes 327712 | tf_op jit(solution)/shard_map/ppermute | solution.py:43
  628.9 5.7 collective-permute-done.43.refs_8_
  636.1 6.3 collective-permute-done.44.refs_9_
  643.3 6.2 collective-permute-done.45.refs_10_
  650.0 6.3 collective-permute-done.46.refs_11_
  656.4 6.8 collective-permute-done.47.refs_12_
  665.4 4.9 place.9.refs_3_.refs_17_
  670.4 4.3 mix.10
  684.2 17.8 %collective-permute-start.72 = (f32[20,8,256]{2,1,0:T(8,128)}, f32[20,8,256]{2,1,0:T(8,128)S(1)}, u32[]{:S(2)}, u32[]{:S(2)}) collective-permute-start(f32[20,8,256]{2,1,0:T(8,128)} %get-tuple-element.196), channel_id=1, source_target_pairs={{0,10},{1,11},{2,8},{3,9},{4,14},{5,15},{6,12},{7,13},{8,2},{9,3},... | collective-permute-start | bytes 491528 | tf_op jit(solution)/shard_map/ppermute | solution.py:43
  705.6 9.6 %collective-permute-start.74 = (f32[20,8,256]{2,1,0:T(8,128)}, f32[20,8,256]{2,1,0:T(8,128)S(1)}, u32[]{:S(2)}, u32[]{:S(2)}) collective-permute-start(f32[20,8,256]{2,1,0:T(8,128)} %get-tuple-element.198), channel_id=1, source_target_pairs={{0,8},{1,9},{2,10},{3,11},{4,12},{5,13},{6,14},{7,15},{8,0},{9,1},... | collective-permute-start | bytes 491528 | tf_op jit(solution)/shard_map/ppermute | solution.py:43
  715.2 4.4 collective-permute-start.75
  719.6 6.3 collective-permute-done.71.refs_5_
  (315 shorter events, 121.3 us)
Async XLA Ops:
  18.9 27.7 %collective-permute-start.1 = (f32[128,8,256]{2,1,0:T(8,128)}, f32[128,8,256]{2,1,0:T(8,128)S(1)}, u32[]{:S(2)}, u32[]{:S(2)}) collective-permute-start(f32[128,8,256]{2,1,0:T(8,128)} %get-tuple-element.117), channel_id=1, source_target_pairs={{0,16},{16,0},{1,17},{17,1},{2,18},{18,2},{3,19},{19,3},{4,20},{20... | collective-permute-start | bytes 3145736 | tf_op jit(solution)/shard_map/ppermute | solution.py:43
  37.7 243.1 %collective-permute-start.51 = (f32[128,8,512]{2,1,0:T(8,128)}, f32[128,8,512]{2,1,0:T(8,128)S(1)}, u32[]{:S(2)}, u32[]{:S(2)}) collective-permute-start(f32[128,8,512]{2,1,0:T(8,128)} %get-tuple-element.174), channel_id=1, source_target_pairs={{0,16},{16,0},{1,17},{17,1},{2,18},{18,2},{3,19},{19,3},{4,20},{20... | collective-permute-start | bytes 6291464 | tf_op jit(solution)/shard_map/ppermute | solution.py:43
  37.7 73.9 %collective-permute-start.5 = (f32[128,8,256]{2,1,0:T(8,128)}, f32[128,8,256]{2,1,0:T(8,128)}, u32[]{:S(2)}, u32[]{:S(2)}) collective-permute-start(f32[128,8,256]{2,1,0:T(8,128)} %get-tuple-element.125), channel_id=1, source_target_pairs={{0,16},{16,0},{1,17},{17,1},{2,18},{18,2},{3,19},{19,3},{4,20},{20... | collective-permute-start | bytes 3145736 | tf_op jit(solution)/shard_map/ppermute | solution.py:43
  39.1 195.1 %collective-permute-start.3 = (f32[128,4,1024]{2,1,0:T(4,128)}, f32[128,4,1024]{2,1,0:T(4,128)}, u32[]{:S(2)}, u32[]{:S(2)}) collective-permute-start(f32[128,4,1024]{2,1,0:T(4,128)} %get-tuple-element.121), channel_id=1, source_target_pairs={{0,1},{1,2},{2,3},{3,4},{4,5},{5,6},{6,7},{7,8},{8,9},{9,10},{10,1... | collective-permute-start | bytes 6291464 | tf_op jit(solution)/shard_map/ppermute | solution.py:351
  52.0 64.3 %collective-permute-start.21 = (f32[20,8,256]{2,1,0:T(8,128)}, f32[20,8,256]{2,1,0:T(8,128)S(1)}, u32[]{:S(2)}, u32[]{:S(2)}) collective-permute-start(f32[20,8,256]{2,1,0:T(8,128)} %get-tuple-element.142), channel_id=1, source_target_pairs={{0,15},{1,14},{2,13},{3,12},{4,11},{5,10},{6,9},{7,8},{8,7},{9,6},... | collective-permute-start | bytes 491528 | tf_op jit(solution)/shard_map/ppermute | solution.py:43
  56.3 60.1 %collective-permute-start.22 = (f32[20,8,256]{2,1,0:T(8,128)}, f32[20,8,256]{2,1,0:T(8,128)S(1)}, u32[]{:S(2)}, u32[]{:S(2)}) collective-permute-start(f32[20,8,256]{2,1,0:T(8,128)} %get-tuple-element.143), channel_id=1, source_target_pairs={{0,14},{1,15},{2,12},{3,13},{4,10},{5,11},{6,8},{7,9},{8,6},{9,7},... | collective-permute-start | bytes 491528 | tf_op jit(solution)/shard_map/ppermute | solution.py:43
  116.3 26.0 %collective-permute-start.25 = (f32[20,8,256]{2,1,0:T(8,128)}, f32[20,8,256]{2,1,0:T(8,128)S(1)}, u32[]{:S(2)}, u32[]{:S(2)}) collective-permute-start(f32[20,8,256]{2,1,0:T(8,128)} %get-tuple-element.146), channel_id=1, source_target_pairs={{0,11},{1,10},{2,9},{3,8},{4,15},{5,14},{6,13},{7,12},{8,3},{9,2},... | collective-permute-start | bytes 491528 | tf_op jit(solution)/shard_map/ppermute | solution.py:43
  120.8 32.0 %collective-permute-start.26 = (f32[20,8,256]{2,1,0:T(8,128)}, f32[20,8,256]{2,1,0:T(8,128)S(1)}, u32[]{:S(2)}, u32[]{:S(2)}) collective-permute-start(f32[20,8,256]{2,1,0:T(8,128)} %get-tuple-element.147), channel_id=1, source_target_pairs={{0,10},{1,11},{2,8},{3,9},{4,14},{5,15},{6,12},{7,13},{8,2},{9,3},... | collective-permute-start | bytes 491528 | tf_op jit(solution)/shard_map/ppermute | solution.py:43
  131.5 167.6 %collective-permute-start = (f32[128,4,1024]{2,1,0:T(4,128)}, f32[128,4,1024]{2,1,0:T(4,128)}, u32[]{:S(2)}, u32[]{:S(2)}) collective-permute-start(f32[128,4,1024]{2,1,0:T(4,128)} %get-tuple-element.115), channel_id=1, source_target_pairs={{1,0},{2,1},{3,2},{4,3},{5,4},{6,5},{7,6},{8,7},{9,8},{10,9},{11,1... | collective-permute-start | bytes 6291464 | tf_op jit(solution)/shard_map/ppermute | solution.py:353
  142.4 38.4 %collective-permute-start.27 = (f32[20,8,256]{2,1,0:T(8,128)}, f32[20,8,256]{2,1,0:T(8,128)S(1)}, u32[]{:S(2)}, u32[]{:S(2)}) collective-permute-start(f32[20,8,256]{2,1,0:T(8,128)} %get-tuple-element.148), channel_id=1, source_target_pairs={{0,9},{1,8},{2,11},{3,10},{4,13},{5,12},{6,15},{7,14},{8,1},{9,0},... | collective-permute-start | bytes 491528 | tf_op jit(solution)/shard_map/ppermute | solution.py:43
  152.8 27.9 %collective-permute-start.28 = (f32[20,8,256]{2,1,0:T(8,128)}, f32[20,8,256]{2,1,0:T(8,128)S(1)}, u32[]{:S(2)}, u32[]{:S(2)}) collective-permute-start(f32[20,8,256]{2,1,0:T(8,128)} %get-tuple-element.149), channel_id=1, source_target_pairs={{0,8},{1,9},{2,10},{3,11},{4,12},{5,13},{6,14},{7,15},{8,0},{9,1},... | collective-permute-start | bytes 491528 | tf_op jit(solution)/shard_map/ppermute | solution.py:43
  206.1 24.8 %collective-permute-start.11 = (f32[20,8,256]{2,1,0:T(8,128)}, f32[20,8,256]{2,1,0:T(8,128)}, u32[]{:S(2)}, u32[]{:S(2)}) collective-permute-start(f32[20,8,256]{2,1,0:T(8,128)} %get-tuple-element.131), channel_id=1, source_target_pairs={{0,10},{1,11},{2,8},{3,9},{4,14},{5,15},{6,12},{7,13},{8,2},{9,3},... | collective-permute-start | bytes 491528 | tf_op jit(solution)/shard_map/ppermute | solution.py:43
  230.9 22.9 %collective-permute-start.13 = (f32[20,8,256]{2,1,0:T(8,128)}, f32[20,8,256]{2,1,0:T(8,128)S(1)}, u32[]{:S(2)}, u32[]{:S(2)}) collective-permute-start(f32[20,8,256]{2,1,0:T(8,128)} %get-tuple-element.133), channel_id=1, source_target_pairs={{0,8},{1,9},{2,10},{3,11},{4,12},{5,13},{6,14},{7,15},{8,0},{9,1},... | collective-permute-start | bytes 491528 | tf_op jit(solution)/shard_map/ppermute | solution.py:43
  234.2 20.9 %collective-permute-start.14 = (f32[20,8,256]{2,1,0:T(8,128)}, f32[20,8,256]{2,1,0:T(8,128)S(1)}, u32[]{:S(2)}, u32[]{:S(2)}) collective-permute-start(f32[20,8,256]{2,1,0:T(8,128)} %get-tuple-element.134), channel_id=1, source_target_pairs={{0,7},{1,6},{2,5},{3,4},{4,3},{5,2},{6,1},{7,0},{8,15},{9,14},{10,... | collective-permute-start | bytes 491528 | tf_op jit(solution)/shard_map/ppermute | solution.py:43
  234.2 21.0 %collective-permute-start.15 = (f32[20,8,256]{2,1,0:T(8,128)}, f32[20,8,256]{2,1,0:T(8,128)S(1)}, u32[]{:S(2)}, u32[]{:S(2)}) collective-permute-start(f32[20,8,256]{2,1,0:T(8,128)} %get-tuple-element.135), channel_id=1, source_target_pairs={{0,6},{1,7},{2,4},{3,5},{4,2},{5,3},{6,0},{7,1},{8,14},{9,15},{10,... | collective-permute-start | bytes 491528 | tf_op jit(solution)/shard_map/ppermute | solution.py:43
  253.8 189.5 %collective-permute-start.4 = (f32[128,8,512]{2,1,0:T(8,128)}, f32[128,8,512]{2,1,0:T(8,128)}, u32[]{:S(2)}, u32[]{:S(2)}) collective-permute-start(f32[128,8,512]{2,1,0:T(8,128)} %get-tuple-element.123), channel_id=1, source_target_pairs={{0,16},{16,0},{1,17},{17,1},{2,18},{18,2},{3,19},{19,3},{4,20},{20... | collective-permute-start | bytes 6291464 | tf_op jit(solution)/shard_map/ppermute | solution.py:43
  274.4 17.2 %collective-permute-start.7 = (f32[20,8,256]{2,1,0:T(8,128)}, f32[20,8,256]{2,1,0:T(8,128)S(1)}, u32[]{:S(2)}, u32[]{:S(2)}) collective-permute-start(f32[20,8,256]{2,1,0:T(8,128)} %get-tuple-element.127), channel_id=1, source_target_pairs={{0,14},{1,15},{2,12},{3,13},{4,10},{5,11},{6,8},{7,9},{8,6},{9,7},... | collective-permute-start | bytes 491528 | tf_op jit(solution)/shard_map/ppermute | solution.py:43
  293.5 45.4 %collective-permute-start.53 = (f32[20,8,512]{2,1,0:T(8,128)}, f32[20,8,512]{2,1,0:T(8,128)S(1)}, u32[]{:S(2)}, u32[]{:S(2)}) collective-permute-start(f32[20,8,512]{2,1,0:T(8,128)} %get-tuple-element.176), channel_id=1, source_target_pairs={{0,14},{1,15},{2,12},{3,13},{4,10},{5,11},{6,8},{7,9},{8,6},{9,7},... | collective-permute-start | bytes 983048 | tf_op jit(solution)/shard_map/ppermute | solution.py:43
  297.2 55.2 %collective-permute-start.54 = (f32[20,8,512]{2,1,0:T(8,128)}, f32[20,8,512]{2,1,0:T(8,128)S(1)}, u32[]{:S(2)}, u32[]{:S(2)}) collective-permute-start(f32[20,8,512]{2,1,0:T(8,128)} %get-tuple-element.177), channel_id=1, source_target_pairs={{0,13},{1,12},{2,15},{3,14},{4,9},{5,8},{6,11},{7,10},{8,5},{9,4},... | collective-permute-start | bytes 983048 | tf_op jit(solution)/shard_map/ppermute | solution.py:43
  299.1 67.0 %collective-permute-start.55 = (f32[20,8,512]{2,1,0:T(8,128)}, f32[20,8,512]{2,1,0:T(8,128)S(1)}, u32[]{:S(2)}, u32[]{:S(2)}) collective-permute-start(f32[20,8,512]{2,1,0:T(8,128)} %get-tuple-element.178), channel_id=1, source_target_pairs={{0,12},{1,13},{2,14},{3,15},{4,8},{5,9},{6,10},{7,11},{8,4},{9,5},... | collective-permute-start | bytes 983048 | tf_op jit(solution)/shard_map/ppermute | solution.py:43
  304.8 92.1 %collective-permute-start.56 = (f32[20,8,512]{2,1,0:T(8,128)}, f32[20,8,512]{2,1,0:T(8,128)S(1)}, u32[]{:S(2)}, u32[]{:S(2)}) collective-permute-start(f32[20,8,512]{2,1,0:T(8,128)} %get-tuple-element.179), channel_id=1, source_target_pairs={{0,11},{1,10},{2,9},{3,8},{4,15},{5,14},{6,13},{7,12},{8,3},{9,2},... | collective-permute-start | bytes 983048 | tf_op jit(solution)/shard_map/ppermute | solution.py:43
  338.9 61.8 %collective-permute-start.57 = (f32[20,8,512]{2,1,0:T(8,128)}, f32[20,8,512]{2,1,0:T(8,128)S(1)}, u32[]{:S(2)}, u32[]{:S(2)}) collective-permute-start(f32[20,8,512]{2,1,0:T(8,128)} %get-tuple-element.180), channel_id=1, source_target_pairs={{0,10},{1,11},{2,8},{3,9},{4,14},{5,15},{6,12},{7,13},{8,2},{9,3},... | collective-permute-start | bytes 983048 | tf_op jit(solution)/shard_map/ppermute | solution.py:43
  352.4 54.5 %collective-permute-start.58 = (f32[20,8,512]{2,1,0:T(8,128)}, f32[20,8,512]{2,1,0:T(8,128)S(1)}, u32[]{:S(2)}, u32[]{:S(2)}) collective-permute-start(f32[20,8,512]{2,1,0:T(8,128)} %get-tuple-element.181), channel_id=1, source_target_pairs={{0,9},{1,8},{2,11},{3,10},{4,13},{5,12},{6,15},{7,14},{8,1},{9,0},... | collective-permute-start | bytes 983048 | tf_op jit(solution)/shard_map/ppermute | solution.py:43
  366.1 48.4 %collective-permute-start.59 = (f32[20,8,512]{2,1,0:T(8,128)}, f32[20,8,512]{2,1,0:T(8,128)}, u32[]{:S(2)}, u32[]{:S(2)}) collective-permute-start(f32[20,8,512]{2,1,0:T(8,128)} %get-tuple-element.182), channel_id=1, source_target_pairs={{0,8},{1,9},{2,10},{3,11},{4,12},{5,13},{6,14},{7,15},{8,0},{9,1},... | collective-permute-start | bytes 983048 | tf_op jit(solution)/shard_map/ppermute | solution.py:43
  397.0 61.7 %collective-permute-start.82 = (f32[128,8,256]{2,1,0:T(8,128)}, f32[128,8,256]{2,1,0:T(8,128)S(1)}, u32[]{:S(2)}, u32[]{:S(2)}) collective-permute-start(f32[128,8,256]{2,1,0:T(8,128)} %get-tuple-element.208), channel_id=1, source_target_pairs={{0,16},{16,0},{1,17},{17,1},{2,18},{18,2},{3,19},{19,3},{4,20},{20... | collective-permute-start | bytes 3145736 | tf_op jit(solution)/shard_map/ppermute | solution.py:43
  400.7 21.1 %collective-permute-start.60 = (f32[20,8,512]{2,1,0:T(8,128)}, f32[20,8,512]{2,1,0:T(8,128)S(1)}, u32[]{:S(2)}, u32[]{:S(2)}) collective-permute-start(f32[20,8,512]{2,1,0:T(8,128)} %get-tuple-element.183), channel_id=1, source_target_pairs={{0,7},{1,6},{2,5},{3,4},{4,3},{5,2},{6,1},{7,0},{8,15},{9,14},{10,... | collective-permute-start | bytes 983048 | tf_op jit(solution)/shard_map/ppermute | solution.py:43
  406.9 21.8 %collective-permute-start.61 = (f32[20,8,512]{2,1,0:T(8,128)}, f32[20,8,512]{2,1,0:T(8,128)S(1)}, u32[]{:S(2)}, u32[]{:S(2)}) collective-permute-start(f32[20,8,512]{2,1,0:T(8,128)} %get-tuple-element.184), channel_id=1, source_target_pairs={{0,6},{1,7},{2,4},{3,5},{4,2},{5,3},{6,0},{7,1},{8,14},{9,15},{10,... | collective-permute-start | bytes 983048 | tf_op jit(solution)/shard_map/ppermute | solution.py:43
  414.5 57.5 %collective-permute-start.2 = (f32[128,8,256]{2,1,0:T(8,128)}, f32[128,8,256]{2,1,0:T(8,128)S(1)}, u32[]{:S(2)}, u32[]{:S(2)}) collective-permute-start(f32[128,8,256]{2,1,0:T(8,128)} %get-tuple-element.120), channel_id=1, source_target_pairs={{0,16},{16,0},{1,17},{17,1},{2,18},{18,2},{3,19},{19,3},{4,20},{20... | collective-permute-start | bytes 3145736 | tf_op jit(solution)/shard_map/ppermute | solution.py:43
  435.6 18.0 %collective-permute-start.64 = (f32[20,8,512]{2,1,0:T(8,128)}, f32[20,8,512]{2,1,0:T(8,128)}, u32[]{:S(2)}, u32[]{:S(2)}) collective-permute-start(f32[20,8,512]{2,1,0:T(8,128)} %get-tuple-element.187), channel_id=1, source_target_pairs={{0,3},{1,2},{2,1},{3,0},{4,7},{5,6},{6,5},{7,4},{8,11},{9,10},{10,... | collective-permute-start | bytes 983048 | tf_op jit(solution)/shard_map/ppermute | solution.py:43
  465.6 23.5 %collective-permute-start.84 = (f32[20,8,256]{2,1,0:T(8,128)}, f32[20,8,256]{2,1,0:T(8,128)S(1)}, u32[]{:S(2)}, u32[]{:S(2)}) collective-permute-start(f32[20,8,256]{2,1,0:T(8,128)} %get-tuple-element.210), channel_id=1, source_target_pairs={{0,14},{1,15},{2,12},{3,13},{4,10},{5,11},{6,8},{7,9},{8,6},{9,7},... | collective-permute-start | bytes 491528 | tf_op jit(solution)/shard_map/ppermute | solution.py:43
  468.1 24.8 %collective-permute-start.85 = (f32[20,8,256]{2,1,0:T(8,128)}, f32[20,8,256]{2,1,0:T(8,128)S(1)}, u32[]{:S(2)}, u32[]{:S(2)}) collective-permute-start(f32[20,8,256]{2,1,0:T(8,128)} %get-tuple-element.211), channel_id=1, source_target_pairs={{0,13},{1,12},{2,15},{3,14},{4,9},{5,8},{6,11},{7,10},{8,5},{9,4},... | collective-permute-start | bytes 491528 | tf_op jit(solution)/shard_map/ppermute | solution.py:43
  470.1 32.1 %collective-permute-start.86 = (f32[20,8,256]{2,1,0:T(8,128)}, f32[20,8,256]{2,1,0:T(8,128)S(1)}, u32[]{:S(2)}, u32[]{:S(2)}) collective-permute-start(f32[20,8,256]{2,1,0:T(8,128)} %get-tuple-element.212), channel_id=1, source_target_pairs={{0,12},{1,13},{2,14},{3,15},{4,8},{5,9},{6,10},{7,11},{8,4},{9,5},... | collective-permute-start | bytes 491528 | tf_op jit(solution)/shard_map/ppermute | solution.py:43
  472.0 40.9 %collective-permute-start.87 = (f32[20,8,256]{2,1,0:T(8,128)}, f32[20,8,256]{2,1,0:T(8,128)S(1)}, u32[]{:S(2)}, u32[]{:S(2)}) collective-permute-start(f32[20,8,256]{2,1,0:T(8,128)} %get-tuple-element.213), channel_id=1, source_target_pairs={{0,11},{1,10},{2,9},{3,8},{4,15},{5,14},{6,13},{7,12},{8,3},{9,2},... | collective-permute-start | bytes 491528 | tf_op jit(solution)/shard_map/ppermute | solution.py:43
  473.5 41.8 %collective-permute-start.88 = (f32[20,8,256]{2,1,0:T(8,128)}, f32[20,8,256]{2,1,0:T(8,128)S(1)}, u32[]{:S(2)}, u32[]{:S(2)}) collective-permute-start(f32[20,8,256]{2,1,0:T(8,128)} %get-tuple-element.214), channel_id=1, source_target_pairs={{0,10},{1,11},{2,8},{3,9},{4,14},{5,15},{6,12},{7,13},{8,2},{9,3},... | collective-permute-start | bytes 491528 | tf_op jit(solution)/shard_map/ppermute | solution.py:43
  489.1 30.5 %collective-permute-start.89 = (f32[20,8,256]{2,1,0:T(8,128)}, f32[20,8,256]{2,1,0:T(8,128)S(1)}, u32[]{:S(2)}, u32[]{:S(2)}) collective-permute-start(f32[20,8,256]{2,1,0:T(8,128)} %get-tuple-element.215), channel_id=1, source_target_pairs={{0,9},{1,8},{2,11},{3,10},{4,13},{5,12},{6,15},{7,14},{8,1},{9,0},... | collective-permute-start | bytes 491528 | tf_op jit(solution)/shard_map/ppermute | solution.py:43
  492.9 43.2 %collective-permute-start.90 = (f32[20,8,256]{2,1,0:T(8,128)}, f32[20,8,256]{2,1,0:T(8,128)S(1)}, u32[]{:S(2)}, u32[]{:S(2)}) collective-permute-start(f32[20,8,256]{2,1,0:T(8,128)} %get-tuple-element.216), channel_id=1, source_target_pairs={{0,8},{1,9},{2,10},{3,11},{4,12},{5,13},{6,14},{7,15},{8,0},{9,1},... | collective-permute-start | bytes 491528 | tf_op jit(solution)/shard_map/ppermute | solution.py:43
  502.3 37.9 %collective-permute-start.91 = (f32[20,8,256]{2,1,0:T(8,128)}, f32[20,8,256]{2,1,0:T(8,128)S(1)}, u32[]{:S(2)}, u32[]{:S(2)}) collective-permute-start(f32[20,8,256]{2,1,0:T(8,128)} %get-tuple-element.217), channel_id=1, source_target_pairs={{0,7},{1,6},{2,5},{3,4},{4,3},{5,2},{6,1},{7,0},{8,15},{9,14},{10,... | collective-permute-start | bytes 491528 | tf_op jit(solution)/shard_map/ppermute | solution.py:43
  512.9 28.8 %collective-permute-start.92 = (f32[20,8,256]{2,1,0:T(8,128)}, f32[20,8,256]{2,1,0:T(8,128)S(1)}, u32[]{:S(2)}, u32[]{:S(2)}) collective-permute-start(f32[20,8,256]{2,1,0:T(8,128)} %get-tuple-element.218), channel_id=1, source_target_pairs={{0,6},{1,7},{2,4},{3,5},{4,2},{5,3},{6,0},{7,1},{8,14},{9,15},{10,... | collective-permute-start | bytes 491528 | tf_op jit(solution)/shard_map/ppermute | solution.py:43
  515.3 27.6 %collective-permute-start.36 = (f32[20,8,512]{2,1,0:T(8,128)S(1)}, f32[20,8,512]{2,1,0:T(8,128)S(1)}, u32[]{:S(2)}, u32[]{:S(2)}) collective-permute-start(f32[20,8,512]{2,1,0:T(8,128)S(1)} %copy-done.68), channel_id=1, source_target_pairs={{0,15},{1,14},{2,13},{3,12},{4,11},{5,10},{6,9},{7,8},{8,7},{9,6},... | collective-permute-start | bytes 983048 | tf_op jit(solution)/shard_map/ppermute | solution.py:43
  519.6 46.8 %collective-permute-start.37 = (f32[20,8,512]{2,1,0:T(8,128)S(1)}, f32[20,8,512]{2,1,0:T(8,128)S(1)}, u32[]{:S(2)}, u32[]{:S(2)}) collective-permute-start(f32[20,8,512]{2,1,0:T(8,128)S(1)} %copy-done.67), channel_id=1, source_target_pairs={{0,14},{1,15},{2,12},{3,13},{4,10},{5,11},{6,8},{7,9},{8,6},{9,7},... | collective-permute-start | bytes 983048 | tf_op jit(solution)/shard_map/ppermute | solution.py:43
  536.1 44.6 %collective-permute-start.38 = (f32[20,8,512]{2,1,0:T(8,128)}, f32[20,8,512]{2,1,0:T(8,128)S(1)}, u32[]{:S(2)}, u32[]{:S(2)}) collective-permute-start(f32[20,8,512]{2,1,0:T(8,128)} %get-tuple-element.159), channel_id=1, source_target_pairs={{0,13},{1,12},{2,15},{3,14},{4,9},{5,8},{6,11},{7,10},{8,5},{9,4},... | collective-permute-start | bytes 983048 | tf_op jit(solution)/shard_map/ppermute | solution.py:43
  540.8 52.8 %collective-permute-start.39 = (f32[20,8,512]{2,1,0:T(8,128)}, f32[20,8,512]{2,1,0:T(8,128)S(1)}, u32[]{:S(2)}, u32[]{:S(2)}) collective-permute-start(f32[20,8,512]{2,1,0:T(8,128)} %get-tuple-element.160), channel_id=1, source_target_pairs={{0,12},{1,13},{2,14},{3,15},{4,8},{5,9},{6,10},{7,11},{8,4},{9,5},... | collective-permute-start | bytes 983048 | tf_op jit(solution)/shard_map/ppermute | solution.py:43
  542.4 72.4 %collective-permute-start.40 = (f32[20,8,512]{2,1,0:T(8,128)}, f32[20,8,512]{2,1,0:T(8,128)S(1)}, u32[]{:S(2)}, u32[]{:S(2)}) collective-permute-start(f32[20,8,512]{2,1,0:T(8,128)} %get-tuple-element.161), channel_id=1, source_target_pairs={{0,11},{1,10},{2,9},{3,8},{4,15},{5,14},{6,13},{7,12},{8,3},{9,2},... | collective-permute-start | bytes 983048 | tf_op jit(solution)/shard_map/ppermute | solution.py:43
  542.9 77.8 %collective-permute-start.41 = (f32[20,8,512]{2,1,0:T(8,128)}, f32[20,8,512]{2,1,0:T(8,128)S(1)}, u32[]{:S(2)}, u32[]{:S(2)}) collective-permute-start(f32[20,8,512]{2,1,0:T(8,128)} %get-tuple-element.162), channel_id=1, source_target_pairs={{0,10},{1,11},{2,8},{3,9},{4,14},{5,15},{6,12},{7,13},{8,2},{9,3},... | collective-permute-start | bytes 983048 | tf_op jit(solution)/shard_map/ppermute | solution.py:43
  566.4 62.4 %collective-permute-start.42 = (f32[20,8,512]{2,1,0:T(8,128)}, f32[20,8,512]{2,1,0:T(8,128)S(1)}, u32[]{:S(2)}, u32[]{:S(2)}) collective-permute-start(f32[20,8,512]{2,1,0:T(8,128)} %get-tuple-element.163), channel_id=1, source_target_pairs={{0,9},{1,8},{2,11},{3,10},{4,13},{5,12},{6,15},{7,14},{8,1},{9,0},... | collective-permute-start | bytes 983048 | tf_op jit(solution)/shard_map/ppermute | solution.py:43
  580.7 53.8 %collective-permute-start.43 = (f32[20,8,512]{2,1,0:T(8,128)}, f32[20,8,512]{2,1,0:T(8,128)}, u32[]{:S(2)}, u32[]{:S(2)}) collective-permute-start(f32[20,8,512]{2,1,0:T(8,128)} %get-tuple-element.164), channel_id=1, source_target_pairs={{0,8},{1,9},{2,10},{3,11},{4,12},{5,13},{6,14},{7,15},{8,0},{9,1},... | collective-permute-start | bytes 983048 | tf_op jit(solution)/shard_map/ppermute | solution.py:43
  593.6 48.8 %collective-permute-start.44 = (f32[20,8,512]{2,1,0:T(8,128)}, f32[20,8,512]{2,1,0:T(8,128)}, u32[]{:S(2)}, u32[]{:S(2)}) collective-permute-start(f32[20,8,512]{2,1,0:T(8,128)} %get-tuple-element.165), channel_id=1, source_target_pairs={{0,7},{1,6},{2,5},{3,4},{4,3},{5,2},{6,1},{7,0},{8,15},{9,14},{10,... | collective-permute-start | bytes 983048 | tf_op jit(solution)/shard_map/ppermute | solution.py:43
  614.8 34.7 %collective-permute-start.45 = (f32[20,8,512]{2,1,0:T(8,128)}, f32[20,8,512]{2,1,0:T(8,128)}, u32[]{:S(2)}, u32[]{:S(2)}) collective-permute-start(f32[20,8,512]{2,1,0:T(8,128)} %get-tuple-element.166), channel_id=1, source_target_pairs={{0,6},{1,7},{2,4},{3,5},{4,2},{5,3},{6,0},{7,1},{8,14},{9,15},{10,... | collective-permute-start | bytes 983048 | tf_op jit(solution)/shard_map/ppermute | solution.py:43
  620.7 35.7 %collective-permute-start.46 = (f32[20,8,512]{2,1,0:T(8,128)}, f32[20,8,512]{2,1,0:T(8,128)}, u32[]{:S(2)}, u32[]{:S(2)}) collective-permute-start(f32[20,8,512]{2,1,0:T(8,128)} %get-tuple-element.167), channel_id=1, source_target_pairs={{0,5},{1,4},{2,7},{3,6},{4,1},{5,0},{6,3},{7,2},{8,13},{9,12},{10,... | collective-permute-start | bytes 983048 | tf_op jit(solution)/shard_map/ppermute | solution.py:43
  628.9 34.3 %collective-permute-start.47 = (f32[20,8,512]{2,1,0:T(8,128)}, f32[20,8,512]{2,1,0:T(8,128)}, u32[]{:S(2)}, u32[]{:S(2)}) collective-permute-start(f32[20,8,512]{2,1,0:T(8,128)} %get-tuple-element.168), channel_id=1, source_target_pairs={{0,4},{1,5},{2,6},{3,7},{4,0},{5,1},{6,2},{7,3},{8,12},{9,13},{10,... | collective-permute-start | bytes 983048 | tf_op jit(solution)/shard_map/ppermute | solution.py:43
  634.5 28.7 %collective-permute-start.48 = (f32[20,8,512]{2,1,0:T(8,128)}, f32[20,8,512]{2,1,0:T(8,128)}, u32[]{:S(2)}, u32[]{:S(2)}) collective-permute-start(f32[20,8,512]{2,1,0:T(8,128)} %get-tuple-element.169), channel_id=1, source_target_pairs={{0,3},{1,2},{2,1},{3,0},{4,7},{5,6},{6,5},{7,4},{8,11},{9,10},{10,... | collective-permute-start | bytes 983048 | tf_op jit(solution)/shard_map/ppermute | solution.py:43
  642.4 21.8 %collective-permute-start.49 = (f32[20,8,512]{2,1,0:T(8,128)}, f32[20,8,512]{2,1,0:T(8,128)}, u32[]{:S(2)}, u32[]{:S(2)}) collective-permute-start(f32[20,8,512]{2,1,0:T(8,128)} %get-tuple-element.170), channel_id=1, source_target_pairs={{0,2},{1,3},{2,0},{3,1},{4,6},{5,7},{6,4},{7,5},{8,10},{9,11},{10,... | collective-permute-start | bytes 983048 | tf_op jit(solution)/shard_map/ppermute | solution.py:43
  656.4 18.3 %collective-permute-start.93 = (f32[20,8,256]{2,1,0:T(8,128)}, f32[20,8,256]{2,1,0:T(8,128)}, u32[]{:S(2)}, u32[]{:S(2)}) collective-permute-start(f32[20,8,256]{2,1,0:T(8,128)} %get-tuple-element.219), channel_id=1, source_target_pairs={{0,5},{1,4},{2,7},{3,6},{4,1},{5,0},{6,3},{7,2},{8,13},{9,12},{10,... | collective-permute-start | bytes 491528 | tf_op jit(solution)/shard_map/ppermute | solution.py:43
  664.3 16.4 %collective-permute-start.96 = (f32[20,8,256]{2,1,0:T(8,128)}, f32[20,8,256]{2,1,0:T(8,128)}, u32[]{:S(2)}, u32[]{:S(2)}) collective-permute-start(f32[20,8,256]{2,1,0:T(8,128)} %get-tuple-element.222), channel_id=1, source_target_pairs={{0,2},{1,3},{2,0},{3,1},{4,6},{5,7},{6,4},{7,5},{8,10},{9,11},{10,... | collective-permute-start | bytes 491528 | tf_op jit(solution)/shard_map/ppermute | solution.py:43
  665.1 17.6 %collective-permute-start.97 = (f32[20,8,256]{2,1,0:T(8,128)}, f32[20,8,256]{2,1,0:T(8,128)}, u32[]{:S(2)}, u32[]{:S(2)}) collective-permute-start(f32[20,8,256]{2,1,0:T(8,128)} %get-tuple-element.223), channel_id=1, source_target_pairs={{0,1},{1,0},{2,3},{3,2},{4,5},{5,4},{6,7},{7,6},{8,9},{9,8},{10,11... | collective-permute-start | bytes 491528 | tf_op jit(solution)/shard_map/ppermute | solution.py:43
  676.7 25.4 %collective-permute-start.68 = (f32[20,8,256]{2,1,0:T(8,128)}, f32[20,8,256]{2,1,0:T(8,128)S(1)}, u32[]{:S(2)}, u32[]{:S(2)}) collective-permute-start(f32[20,8,256]{2,1,0:T(8,128)} %get-tuple-element.192), channel_id=1, source_target_pairs={{0,14},{1,15},{2,12},{3,13},{4,10},{5,11},{6,8},{7,9},{8,6},{9,7},... | collective-permute-start | bytes 491528 | tf_op jit(solution)/shard_map/ppermute | solution.py:43
  679.1 26.4 %collective-permute-start.69 = (f32[20,8,256]{2,1,0:T(8,128)}, f32[20,8,256]{2,1,0:T(8,128)S(1)}, u32[]{:S(2)}, u32[]{:S(2)}) collective-permute-start(f32[20,8,256]{2,1,0:T(8,128)} %get-tuple-element.193), channel_id=1, source_target_pairs={{0,13},{1,12},{2,15},{3,14},{4,9},{5,8},{6,11},{7,10},{8,5},{9,4},... | collective-permute-start | bytes 491528 | tf_op jit(solution)/shard_map/ppermute | solution.py:43
  680.6 34.5 %collective-permute-start.70 = (f32[20,8,256]{2,1,0:T(8,128)}, f32[20,8,256]{2,1,0:T(8,128)S(1)}, u32[]{:S(2)}, u32[]{:S(2)}) collective-permute-start(f32[20,8,256]{2,1,0:T(8,128)} %get-tuple-element.194), channel_id=1, source_target_pairs={{0,12},{1,13},{2,14},{3,15},{4,8},{5,9},{6,10},{7,11},{8,4},{9,5},... | collective-permute-start | bytes 491528 | tf_op jit(solution)/shard_map/ppermute | solution.py:43
  682.7 43.1 %collective-permute-start.71 = (f32[20,8,256]{2,1,0:T(8,128)}, f32[20,8,256]{2,1,0:T(8,128)S(1)}, u32[]{:S(2)}, u32[]{:S(2)}) collective-permute-start(f32[20,8,256]{2,1,0:T(8,128)} %get-tuple-element.195), channel_id=1, source_target_pairs={{0,11},{1,10},{2,9},{3,8},{4,15},{5,14},{6,13},{7,12},{8,3},{9,2},... | collective-permute-start | bytes 491528 | tf_op jit(solution)/shard_map/ppermute | solution.py:43
  684.2 45.0 %collective-permute-start.72 = (f32[20,8,256]{2,1,0:T(8,128)}, f32[20,8,256]{2,1,0:T(8,128)S(1)}, u32[]{:S(2)}, u32[]{:S(2)}) collective-permute-start(f32[20,8,256]{2,1,0:T(8,128)} %get-tuple-element.196), channel_id=1, source_target_pairs={{0,10},{1,11},{2,8},{3,9},{4,14},{5,15},{6,12},{7,13},{8,2},{9,3},... | collective-permute-start | bytes 491528 | tf_op jit(solution)/shard_map/ppermute | solution.py:43
  702.0 30.5 %collective-permute-start.73 = (f32[20,8,256]{2,1,0:T(8,128)}, f32[20,8,256]{2,1,0:T(8,128)S(1)}, u32[]{:S(2)}, u32[]{:S(2)}) collective-permute-start(f32[20,8,256]{2,1,0:T(8,128)} %get-tuple-element.197), channel_id=1, source_target_pairs={{0,9},{1,8},{2,11},{3,10},{4,13},{5,12},{6,15},{7,14},{8,1},{9,0},... | collective-permute-start | bytes 491528 | tf_op jit(solution)/shard_map/ppermute | solution.py:43
  705.6 30.1 %collective-permute-start.74 = (f32[20,8,256]{2,1,0:T(8,128)}, f32[20,8,256]{2,1,0:T(8,128)S(1)}, u32[]{:S(2)}, u32[]{:S(2)}) collective-permute-start(f32[20,8,256]{2,1,0:T(8,128)} %get-tuple-element.198), channel_id=1, source_target_pairs={{0,8},{1,9},{2,10},{3,11},{4,12},{5,13},{6,14},{7,15},{8,0},{9,1},... | collective-permute-start | bytes 491528 | tf_op jit(solution)/shard_map/ppermute | solution.py:43
  715.2 23.1 %collective-permute-start.75 = (f32[20,8,256]{2,1,0:T(8,128)}, f32[20,8,256]{2,1,0:T(8,128)S(1)}, u32[]{:S(2)}, u32[]{:S(2)}) collective-permute-start(f32[20,8,256]{2,1,0:T(8,128)} %get-tuple-element.199), channel_id=1, source_target_pairs={{0,7},{1,6},{2,5},{3,4},{4,3},{5,2},{6,1},{7,0},{8,15},{9,14},{10,... | collective-permute-start | bytes 491528 | tf_op jit(solution)/shard_map/ppermute | solution.py:43
  729.2 16.2 %collective-permute-start.77 = (f32[20,8,256]{2,1,0:T(8,128)}, f32[20,8,256]{2,1,0:T(8,128)S(1)}, u32[]{:S(2)}, u32[]{:S(2)}) collective-permute-start(f32[20,8,256]{2,1,0:T(8,128)} %get-tuple-element.201), channel_id=1, source_target_pairs={{0,5},{1,4},{2,7},{3,6},{4,1},{5,0},{6,3},{7,2},{8,13},{9,12},{10,... | collective-permute-start | bytes 491528 | tf_op jit(solution)/shard_map/ppermute | solution.py:43
  (111 other events, 2947.9 us)
